TPU v7x, 128 devices: a whole 4x4x4 slice. The times are simulated.
128 devices in a mesh: rows: 64 (over y, z, x), cols: 2 (over core).
Axes of the slice: x: 4, y: 4, z: 4, core: 2. Of those that a mesh axis runs over, the one named last changes fastest.
Arguments:
- video: bfloat16 [512, 256, 256], P('rows', 'cols'), may hold values from -12 to 12
- foreground: float32 [512, 256, 256], P('rows', 'cols'), may hold values from -4 to 4
- scaled_dual: float32 [512, 256, 256], P('rows', 'cols'), may hold values from -2.5 to 2.5
Outputs:
- background: float32 [512, 256, 256], P('rows', 'cols')
- new_foreground: float32 [512, 256, 256], P('rows', 'cols')
- new_dual: float32 [512, 256, 256], P('rows', 'cols')
All inputs are finite; a program needn't handle non-finite values.
Results may differ from a plain program's by a relative error of at most 0.00035.
Values sent between devices are 32-bit elements; how exact they have to be, the bound alone decides.
A program may use at most 64 MiB of HBM per device.

v0:
```python
import jax
import jax.numpy as jnp
from jax import lax
from jax.sharding import PartitionSpec as P
from jax.experimental import pallas as pl
from jax.experimental.pallas import tpu as pltpu


K_ROOT = 8
K_SIGN = 6
K_TV = 8


threshold_ratio = 1.0
dual_step = 0.25
tv_weight = 1.0

HALO = K_TV


def shifted(x, axis, by):
    length = lax.axis_size(axis)
    pairs = [(i, i + by) for i in range(length) if 0 <= i + by < length]
    return lax.ppermute(x, axis, pairs)


def matmul(left, right):
    return jnp.dot(left, right, precision=lax.Precision.HIGH, preferred_element_type=jnp.float32)


def shrink_matrix(gram):
    size = gram.shape[0]
    identity = jnp.eye(size, dtype=jnp.float32)
    scale = jnp.sqrt(jnp.sum(gram * gram))
    root = gram / scale
    inverse = identity
    for _ in range(K_ROOT):
        factor = 1.5 * identity - 0.5 * matmul(inverse, root)
        root = matmul(root, factor)
        inverse = matmul(factor, inverse)
    cutoff = threshold_ratio * jnp.trace(root) / size
    signed = root - cutoff * identity
    for _ in range(K_SIGN):
        signed = 1.5 * signed - 0.5 * matmul(signed, matmul(signed, signed))
    return 0.5 * matmul(identity - cutoff * inverse, identity + signed)


def halo_pieces(block):
    up = shifted(block[-HALO:], "rows", 1)
    down = shifted(block[:HALO], "rows", -1)
    left = shifted(jnp.concatenate([up[:, -HALO:], block[:, -HALO:], down[:, -HALO:]], axis=0), "cols", 1)
    right = shifted(jnp.concatenate([up[:, :HALO], block[:, :HALO], down[:, :HALO]], axis=0), "cols", -1)
    return up, block, down, left, right


def all_sum(x):
    for axis in ("cols", "rows"):
        length = lax.axis_size(axis)
        if length & (length - 1):
            x = lax.psum(x, axis)
            continue
        groups, step = [], 1
        while step < length:
            radix = 4 if 4 * step <= length else 2
            groups.append((step, radix))
            step *= radix
        for step, radix in groups:
            if radix == 4:
                r1, r2, r3 = (lax.ppermute(x, axis, [(i, i ^ (k * step)) for i in range(length)]) for k in (1, 2, 3))
                x = (x + r1) + (r2 + r3)
            else:
                x = x + lax.ppermute(x, axis, [(i, i ^ step) for i in range(length)])
    return x


def summed_gram(flat):
    local = matmul(flat.T, flat)
    half = local.shape[0] // 2
    packed = all_sum(jnp.concatenate([local[:half], local[half:, half:]], axis=1))
    top = packed[:, : 2 * half]
    corner = packed[:, 2 * half :]
    bottom = jnp.concatenate([top[:, half:].T, corner], axis=1)
    return jnp.concatenate([top, bottom], axis=0)


def tv_kernel(up_ref, mid_ref, down_ref, left_ref, right_ref, kx_ref, ky_ref, fg_ref, dual_ref):
    t = jnp.concatenate([up_ref[...], mid_ref[...], down_ref[...]], axis=0)
    t = jnp.concatenate([left_ref[...], t, right_ref[...]], axis=1)
    rows, cols = t.shape[0], t.shape[1]
    kx = kx_ref[...]
    ky = ky_ref[...][None]

    def prev_y(q):
        return pltpu.roll(q, 1, 1)

    def next_y(q):
        return pltpu.roll(q, cols - 1, 1)

    s = t
    px = jnp.clip(dual_step * (s[1:] - s[:-1]), -tv_weight, tv_weight) * kx[: rows - 1]
    py = jnp.clip(dual_step * (next_y(s[: rows - 1]) - s[: rows - 1]), -tv_weight, tv_weight) * ky
    for sweep in range(2, K_TV + 1):
        n = rows + 3 - 2 * sweep
        q = py[1:n]
        s = t[sweep - 1 : rows + 1 - sweep] - (px[: n - 1] - px[1:n] + prev_y(q) - q)
        down = s[1:] - s[:-1]
        across = next_y(s[:-1]) - s[:-1]
        px = jnp.clip(px[1 : n - 1] + dual_step * down, -tv_weight, tv_weight) * kx[sweep - 1 : rows - sweep]
        py = jnp.clip(py[1 : n - 1] + dual_step * across, -tv_weight, tv_weight) * ky
    q = py[1:]
    inner = rows - 2 * HALO
    middle = t[HALO : HALO + inner]
    fg = middle - (px[:-1] - px[1:] + prev_y(q) - q)
    width = cols - 2 * HALO
    fg = fg[:, HALO : HALO + width]
    fg_ref[...] = fg
    dual_ref[...] = middle[:, HALO : HALO + width] - fg


def tv_local(pieces, kx, ky, chunk, frames, into=None):
    up, mid, down, left, right = pieces
    inner_rows, inner_cols, lanes = mid.shape
    rows, cols = inner_rows + 2 * HALO, inner_cols + 2 * HALO
    out = jax.ShapeDtypeStruct((inner_rows, inner_cols, frames), jnp.float32)

    def whole(shape):
        return pl.BlockSpec(shape, lambda f: (0,) * len(shape))

    in_specs = [whole(up.shape), whole(mid.shape), whole(down.shape), whole(left.shape), whole(right.shape)]
    in_specs += [whole((rows, 1, lanes)), whole((cols, lanes))]
    operands = [up, mid, down, left, right, kx, ky]
    aliases = {}
    body = tv_kernel
    if into is not None:
        in_specs += [pl.BlockSpec(memory_space=pl.ANY), pl.BlockSpec(memory_space=pl.ANY)]
        operands += list(into)
        aliases = {7: 0, 8: 1}

        def body(*refs):
            tv_kernel(*refs[:7], *refs[9:])

    return pl.pallas_call(
        body,
        grid=(1,),
        in_specs=in_specs,
        out_specs=[
            pl.BlockSpec((inner_rows, inner_cols, lanes), lambda f: (0, 0, chunk)),
            pl.BlockSpec((inner_rows, inner_cols, lanes), lambda f: (0, 0, chunk)),
        ],
        out_shape=[out, out],
        input_output_aliases=aliases,
    )(*operands)


def per_device(video, foreground, scaled_dual):
    rows_here, cols_here, frames = foreground.shape
    total_rows = rows_here * lax.axis_size("rows")
    total_cols = cols_here * lax.axis_size("cols")
    observed = video.astype(jnp.float32)
    mixed = observed - foreground + scaled_dual
    flat = mixed.reshape(-1, frames)
    gram = summed_gram(flat)
    shrink = shrink_matrix(gram)
    background = matmul(flat, shrink).reshape(foreground.shape)
    target = observed - background + scaled_dual
    ext_rows, ext_cols = rows_here + 2 * HALO, cols_here + 2 * HALO

    first_row = lax.axis_index("rows") * rows_here - HALO
    first_col = lax.axis_index("cols") * cols_here - HALO
    g = first_row + lax.broadcasted_iota(jnp.int32, (ext_rows, 1, 1), 0)
    h = first_col + lax.broadcasted_iota(jnp.int32, (1, ext_cols, 1), 1)
    lanes = 128 if frames % 128 == 0 else frames
    keep_x = (g >= 0) & (g <= total_rows - 2)
    keep_y = (h >= 0) & (h <= total_cols - 2)
    kx = jnp.broadcast_to(jnp.where(keep_x, 1.0, 0.0).astype(jnp.float32), (ext_rows, 1, lanes))
    ky = jnp.broadcast_to(jnp.where(keep_y, 1.0, 0.0).astype(jnp.float32)[0], (ext_cols, lanes))
    outs = None
    for chunk in range(frames // lanes):
        pieces = halo_pieces(target[:, :, chunk * lanes : (chunk + 1) * lanes])
        outs = tv_local(pieces, kx, ky, chunk, frames, outs)
    new_foreground, new_dual = outs
    return (background, new_foreground, new_dual)


def solution(mesh):
    return jax.shard_map(
        per_device,
        mesh=mesh,
        in_specs=(P("rows", "cols", None), P("rows", "cols", None), P("rows", "cols", None)),
        out_specs=(P("rows", "cols", None), P("rows", "cols", None), P("rows", "cols", None)),
        check_vma=False,
    )
```

profile of v0, /device:TPU:8, one launch (start us, length us, event | category | flops | bytes accessed | tf_op | source)
XLA Modules:
  0.0 119.9 jit_solution(12504169672467180477)
XLA Ops:
  0.6 3.5 %convolution_bitcast_fusion = f32[256,256]{0,1:T(8,128)S(1)} fusion(f32[8,128,256]{2,1,0:T(8,128)} %param.5, f32[8,128,256]{2,1,0:T(8,128)} %param.4, bf16[8,128,256]{2,1,0:T(8,128)(2,1)} %param.3), kind=kOutput, calls=%fused_computation.35 | convolution fusion | flops 403439616 | bytes 2883584 | tf_op jit(solution)/shard_map/dot_general | solution.py:28
  4.3 1.4 %collective-permute-done = f32[128,384]{0,1:T(8,128)S(1)} collective-permute-done((f32[128,384]{0,1:T(8,128)S(1)}, f32[128,384]{0,1:T(8,128)S(1)}, u32[]{:S(2)}, u32[]{:S(2)}) %collective-permute-start) | collective-permute-done | bytes 196640 | tf_op jit(solution)/shard_map/ppermute | solution.py:72
  5.8 2.8 %collective-permute-start.3 = (f32[128,384]{0,1:T(8,128)S(1)}, f32[128,384]{0,1:T(8,128)S(1)}, u32[]{:S(2)}, u32[]{:S(2)}) collective-permute-start(f32[128,384]{0,1:T(8,128)S(1)} %fusion.36), channel_id=1, source_target_pairs={{0,6},{2,4},{4,2},{6,0},{8,14},{10,12},{12,10},{14,8},{16,22},{18,... | collective-permute-start | bytes 589832 | tf_op jit(solution)/shard_map/ppermute | solution.py:69
  8.6 0.8 collective-permute-start.2
  9.4 0.5 collective-permute-start.1
  9.9 8.3 %collective-permute-done.3 = f32[128,384]{0,1:T(8,128)S(1)} collective-permute-done((f32[128,384]{0,1:T(8,128)S(1)}, f32[128,384]{0,1:T(8,128)S(1)}, u32[]{:S(2)}, u32[]{:S(2)}) %collective-permute-start.3) | collective-permute-done | bytes 196640 | tf_op jit(solution)/shard_map/ppermute | solution.py:69
  18.2 0.6 collective-permute-done.1
  18.9 4.1 %collective-permute-start.6 = (f32[128,384]{0,1:T(8,128)S(1)}, f32[128,384]{0,1:T(8,128)S(1)}, u32[]{:S(2)}, u32[]{:S(2)}) collective-permute-start(f32[128,384]{0,1:T(8,128)S(1)} %add_add_fusion.2), channel_id=1, source_target_pairs={{0,24},{2,26},{4,28},{6,30},{8,16},{10,18},{12,20},{14,22},{16,8},... | collective-permute-start | bytes 589832 | tf_op jit(solution)/shard_map/ppermute | solution.py:69
  23.0 0.9 collective-permute-start.4
  24.0 6.6 %collective-permute-done.6 = f32[128,384]{0,1:T(8,128)S(1)} collective-permute-done((f32[128,384]{0,1:T(8,128)S(1)}, f32[128,384]{0,1:T(8,128)S(1)}, u32[]{:S(2)}, u32[]{:S(2)}) %collective-permute-start.6) | collective-permute-done | bytes 196640 | tf_op jit(solution)/shard_map/ppermute | solution.py:69
  30.6 1.6 %collective-permute-done.5 = f32[128,384]{0,1:T(8,128)S(1)} collective-permute-done((f32[128,384]{0,1:T(8,128)S(1)}, f32[128,384]{0,1:T(8,128)S(1)}, u32[]{:S(2)}, u32[]{:S(2)}) %collective-permute-start.5) | collective-permute-done | bytes 196640 | tf_op jit(solution)/shard_map/ppermute | solution.py:69
  32.3 1.7 %collective-permute-start.9 = (f32[128,384]{0,1:T(8,128)S(1)}, f32[128,384]{0,1:T(8,128)S(1)}, u32[]{:S(2)}, u32[]{:S(2)}) collective-permute-start(f32[128,384]{0,1:T(8,128)S(1)} %add_add_fusion.1), channel_id=1, source_target_pairs={{0,96},{2,98},{4,100},{6,102},{8,104},{10,106},{12,108},{14,110},{... | collective-permute-start | bytes 589832 | tf_op jit(solution)/shard_map/ppermute | solution.py:69
  33.9 0.9 collective-permute-start.8
  34.9 1.6 %collective-permute-start.7 = (f32[128,384]{0,1:T(8,128)S(1)}, f32[128,384]{0,1:T(8,128)S(1)}, u32[]{:S(2)}, u32[]{:S(2)}) collective-permute-start(f32[128,384]{0,1:T(8,128)S(1)} %add_add_fusion.1), channel_id=1, source_target_pairs={{0,32},{2,34},{4,36},{6,38},{8,40},{10,42},{12,44},{14,46},{16,48}... | collective-permute-start | bytes 589832 | tf_op jit(solution)/shard_map/ppermute | solution.py:69
  36.5 4.5 %collective-permute-done.9 = f32[128,384]{0,1:T(8,128)S(1)} collective-permute-done((f32[128,384]{0,1:T(8,128)S(1)}, f32[128,384]{0,1:T(8,128)S(1)}, u32[]{:S(2)}, u32[]{:S(2)}) %collective-permute-start.9) | collective-permute-done | bytes 196640 | tf_op jit(solution)/shard_map/ppermute | solution.py:69
  41.0 1.2 collective-permute-done.8
  42.2 1.1 collective-permute-done.7
  43.5 0.7 multiply_reduce_fusion
  44.8 0.3 fusion.15
  45.1 0.4 fusion.29
  45.8 0.3 fusion.14
  46.1 0.3 fusion.45
  46.3 0.3 fusion.44
  46.6 0.3 fusion.13
  46.9 0.3 fusion.47
  47.5 0.3 fusion.12
  47.7 0.3 fusion.49
  48.3 0.3 fusion.11
  48.6 0.3 fusion.51
  49.1 0.3 fusion.10
  50.0 0.3 fusion.9
  51.1 0.9 select_reduce_fusion
  52.9 0.3 fusion.20
  53.2 0.3 fusion.6
  53.5 0.3 fusion.56
  53.8 0.3 fusion.5
  54.0 0.3 fusion.57
  54.3 0.3 fusion.4
  54.6 0.3 fusion.58
  54.9 0.3 fusion.3
  55.2 0.3 fusion.59
  55.5 0.3 fusion.2
  55.8 0.3 fusion.60
  56.1 0.3 fusion.16
  56.3 0.3 fusion
  56.6 0.4 copy-done
  57.0 0.3 copy-done.1
  57.3 1.6 %fusion.18 = (f32[8,128,256]{2,1,0:T(8,128)S(1)}, f32[8,128,256]{2,1,0:T(8,128)}) fusion(f32[8,128,256]{2,1,0:T(8,128)S(1)} %copy-done, bf16[8,128,256]{2,1,0:T(8,128)(2,1)S(1)} %copy-done.2, f32[256,256,1]{1,0,2:T(8,128)S(1)} %fusion, f32[8,128,256]{2,1,0:T(8,128)S(1)} %copy-done.1), kind=kOutput, calls=%fused_computation.37 | convolution fusion | flops 404226048 | bytes 4980736 | tf_op jit(solution)/shard_map/dot_general | solution.py:28
  59.1 7.9 %collective-permute-start.15 = (f32[8,128,128]{2,1,0:T(8,128)S(1)}, f32[8,128,128]{2,1,0:T(8,128)S(1)}, u32[]{:S(2)}, u32[]{:S(2)}) collective-permute-start(f32[8,128,128]{2,1,0:T(8,128)S(1)} %get-tuple-element.15.mid_ref), channel_id=1, source_target_pairs={{2,0},{4,2},{6,4},{8,6},{10,8},{12,10},{14,12},{16,14},{18,16},{20... | collective-permute-start | bytes 1572872 | tf_op jit(solution)/shard_map/ppermute | solution.py:24
  67.0 1.9 %collective-permute-start.14 = (f32[8,128,128]{2,1,0:T(8,128)S(1)}, f32[8,128,128]{2,1,0:T(8,128)S(1)}, u32[]{:S(2)}, u32[]{:S(2)}) collective-permute-start(f32[8,128,128]{2,1,0:T(8,128)S(1)} %get-tuple-element.15.mid_ref), channel_id=1, source_target_pairs={{0,2},{2,4},{4,6},{6,8},{8,10},{10,12},{12,14},{14,16},{16,18},{18... | collective-permute-start | bytes 1572872 | tf_op jit(solution)/shard_map/ppermute | solution.py:24
  69.0 8.1 %collective-permute-start.11 = (f32[8,128,128]{2,1,0:T(8,128)S(1)}, f32[8,128,128]{2,1,0:T(8,128)S(1)}, u32[]{:S(2)}, u32[]{:S(2)}) collective-permute-start(f32[8,128,128]{2,1,0:T(8,128)S(1)} %get-tuple-element.16.refs_1_), channel_id=1, source_target_pairs={{2,0},{4,2},{6,4},{8,6},{10,8},{12,10},{14,12},{16,14},{18,16},{20... | collective-permute-start | bytes 1572872 | tf_op jit(solution)/shard_map/ppermute | solution.py:24
  77.1 1.9 %collective-permute-start.10 = (f32[8,128,128]{2,1,0:T(8,128)S(1)}, f32[8,128,128]{2,1,0:T(8,128)S(1)}, u32[]{:S(2)}, u32[]{:S(2)}) collective-permute-start(f32[8,128,128]{2,1,0:T(8,128)S(1)} %get-tuple-element.16.refs_1_), channel_id=1, source_target_pairs={{0,2},{2,4},{4,6},{6,8},{8,10},{10,12},{12,14},{14,16},{16,18},{18... | collective-permute-start | bytes 1572872 | tf_op jit(solution)/shard_map/ppermute | solution.py:24
  79.1 7.2 %collective-permute-done.14.up_ref = f32[8,128,128]{2,1,0:T(8,128)S(1)} collective-permute-done((f32[8,128,128]{2,1,0:T(8,128)S(1)}, f32[8,128,128]{2,1,0:T(8,128)S(1)}, u32[]{:S(2)}, u32[]{:S(2)}) %collective-permute-start.14) | collective-permute-done | bytes 524320 | tf_op jit(solution)/shard_map/ppermute | solution.py:24
  86.3 1.3 %collective-permute-start.16 = (f32[24,8,128]{2,1,0:T(8,128)S(1)}, f32[24,8,128]{2,1,0:T(8,128)S(1)}, u32[]{:S(2)}, u32[]{:S(2)}) collective-permute-start(f32[24,8,128]{2,1,0:T(8,128)S(1)} %pad_maximum_fusion.3), channel_id=1, source_target_pairs={{0,1},{2,3},{4,5},{6,7},{8,9},{10,11},{12,13},{14,15},{16,17},{18,... | collective-permute-start | bytes 294920 | tf_op jit(solution)/shard_map/ppermute | solution.py:24
  87.6 1.3 %collective-permute-start.17 = (f32[24,8,128]{2,1,0:T(8,128)S(1)}, f32[24,8,128]{2,1,0:T(8,128)S(1)}, u32[]{:S(2)}, u32[]{:S(2)}) collective-permute-start(f32[24,8,128]{2,1,0:T(8,128)S(1)} %pad_maximum_fusion.4), channel_id=1, source_target_pairs={{1,0},{3,2},{5,4},{7,6},{9,8},{11,10},{13,12},{15,14},{17,16},{19,... | collective-permute-start | bytes 294920 | tf_op jit(solution)/shard_map/ppermute | solution.py:24
  89.0 6.8 %collective-permute-done.10.refs_0_ = f32[8,128,128]{2,1,0:T(8,128)S(1)} collective-permute-done((f32[8,128,128]{2,1,0:T(8,128)S(1)}, f32[8,128,128]{2,1,0:T(8,128)S(1)}, u32[]{:S(2)}, u32[]{:S(2)}) %collective-permute-start.10) | collective-permute-done | bytes 524320 | tf_op jit(solution)/shard_map/ppermute | solution.py:24
  95.8 0.8 copy-done.7
  96.6 1.3 %collective-permute-start.12 = (f32[24,8,128]{2,1,0:T(8,128)S(1)}, f32[24,8,128]{2,1,0:T(8,128)S(1)}, u32[]{:S(2)}, u32[]{:S(2)}) collective-permute-start(f32[24,8,128]{2,1,0:T(8,128)S(1)} %pad_maximum_fusion.1), channel_id=1, source_target_pairs={{0,1},{2,3},{4,5},{6,7},{8,9},{10,11},{12,13},{14,15},{16,17},{18,... | collective-permute-start | bytes 294920 | tf_op jit(solution)/shard_map/ppermute | solution.py:24
  98.0 1.5 %collective-permute-start.13 = (f32[24,8,128]{2,1,0:T(8,128)S(1)}, f32[24,8,128]{2,1,0:T(8,128)S(1)}, u32[]{:S(2)}, u32[]{:S(2)}) collective-permute-start(f32[24,8,128]{2,1,0:T(8,128)S(1)} %pad_maximum_fusion.2), channel_id=1, source_target_pairs={{1,0},{3,2},{5,4},{7,6},{9,8},{11,10},{13,12},{15,14},{17,16},{19,... | collective-permute-start | bytes 294920 | tf_op jit(solution)/shard_map/ppermute | solution.py:24
  99.5 0.7 broadcast_in_dim.30.kx_ref.refs_5_
  100.2 0.7 broadcast_in_dim.33.ky_ref.refs_6_
  100.9 9.1 %shard_map.58 = (f32[8,128,256]{2,1,0:T(8,128)}, f32[8,128,256]{2,1,0:T(8,128)}) custom-call(f32[8,128,128]{2,1,0:T(8,128)} %copy-done.8, f32[8,128,128]{2,1,0:T(8,128)} %copy-done.4, f32[8,128,128]{2,1,0:T(8,128)} %copy-done.5, f32[24,8,128]{2,1,0:T(8,128)} %copy-done.9, f32[24,8,128]{2,1,0:T(8,128)} %copy-done.10, ...), custom_call_target="tpu_custom_call" | custom-call | tf_op jit(solution)/shard_map/pallas_call | solution.py:142
  110.1 0.6 copy-done.11
  110.8 9.1 %shard_map.59 = (f32[8,128,256]{2,1,0:T(8,128)}, f32[8,128,256]{2,1,0:T(8,128)}) custom-call(f32[8,128,128]{2,1,0:T(8,128)} %copy-done.7, f32[8,128,128]{2,1,0:T(8,128)} %copy-done.3, f32[8,128,128]{2,1,0:T(8,128)} %copy-done.6, f32[24,8,128]{2,1,0:T(8,128)} %copy-done.11, f32[24,8,128]{2,1,0:T(8,128)} %copy-done.12, ...), custom_call_target="tpu_custom_call", output_to_operand_aliasing={{0}: (7, {}), {1}: (8, {})} | custom-call | tf_op jit(solution)/shard_map/pallas_call | solution.py:142
  (64 shorter events, 3.4 us)
Async XLA Ops:
  4.2 1.5 %collective-permute-start = (f32[128,384]{0,1:T(8,128)S(1)}, f32[128,384]{0,1:T(8,128)S(1)}, u32[]{:S(2)}, u32[]{:S(2)}) collective-permute-start(f32[128,384]{0,1:T(8,128)S(1)} %pad_maximum_fusion), channel_id=1, source_target_pairs={{0,1},{1,0},{2,3},{3,2},{4,5},{5,4},{6,7},{7,6},{8,9},{9,8},{10,11... | collective-permute-start | bytes 589832 | tf_op jit(solution)/shard_map/ppermute | solution.py:72
  5.8 12.4 %collective-permute-start.3 = (f32[128,384]{0,1:T(8,128)S(1)}, f32[128,384]{0,1:T(8,128)S(1)}, u32[]{:S(2)}, u32[]{:S(2)}) collective-permute-start(f32[128,384]{0,1:T(8,128)S(1)} %fusion.36), channel_id=1, source_target_pairs={{0,6},{2,4},{4,2},{6,0},{8,14},{10,12},{12,10},{14,8},{16,22},{18,... | collective-permute-start | bytes 589832 | tf_op jit(solution)/shard_map/ppermute | solution.py:69
  8.6 9.6 %collective-permute-start.2 = (f32[128,384]{0,1:T(8,128)S(1)}, f32[128,384]{0,1:T(8,128)S(1)}, u32[]{:S(2)}, u32[]{:S(2)}) collective-permute-start(f32[128,384]{0,1:T(8,128)S(1)} %fusion.36), channel_id=1, source_target_pairs={{0,4},{2,6},{4,0},{6,2},{8,12},{10,14},{12,8},{14,10},{16,20},{18,... | collective-permute-start | bytes 589832 | tf_op jit(solution)/shard_map/ppermute | solution.py:69
  9.4 9.4 %collective-permute-start.1 = (f32[128,384]{0,1:T(8,128)S(1)}, f32[128,384]{0,1:T(8,128)S(1)}, u32[]{:S(2)}, u32[]{:S(2)}) collective-permute-start(f32[128,384]{0,1:T(8,128)S(1)} %fusion.36), channel_id=1, source_target_pairs={{0,2},{2,0},{4,6},{6,4},{8,10},{10,8},{12,14},{14,12},{16,18},{18,... | collective-permute-start | bytes 589832 | tf_op jit(solution)/shard_map/ppermute | solution.py:69
  18.9 11.7 %collective-permute-start.6 = (f32[128,384]{0,1:T(8,128)S(1)}, f32[128,384]{0,1:T(8,128)S(1)}, u32[]{:S(2)}, u32[]{:S(2)}) collective-permute-start(f32[128,384]{0,1:T(8,128)S(1)} %add_add_fusion.2), channel_id=1, source_target_pairs={{0,24},{2,26},{4,28},{6,30},{8,16},{10,18},{12,20},{14,22},{16,8},... | collective-permute-start | bytes 589832 | tf_op jit(solution)/shard_map/ppermute | solution.py:69
  23.0 9.2 %collective-permute-start.5 = (f32[128,384]{0,1:T(8,128)S(1)}, f32[128,384]{0,1:T(8,128)S(1)}, u32[]{:S(2)}, u32[]{:S(2)}) collective-permute-start(f32[128,384]{0,1:T(8,128)S(1)} %add_add_fusion.2), channel_id=1, source_target_pairs={{0,16},{2,18},{4,20},{6,22},{8,24},{10,26},{12,28},{14,30},{16,0},... | collective-permute-start | bytes 589832 | tf_op jit(solution)/shard_map/ppermute | solution.py:69
  23.0 9.2 %collective-permute-start.4 = (f32[128,384]{0,1:T(8,128)S(1)}, f32[128,384]{0,1:T(8,128)S(1)}, u32[]{:S(2)}, u32[]{:S(2)}) collective-permute-start(f32[128,384]{0,1:T(8,128)S(1)} %add_add_fusion.2), channel_id=1, source_target_pairs={{0,8},{2,10},{4,12},{6,14},{8,0},{10,2},{12,4},{14,6},{16,24},{18,... | collective-permute-start | bytes 589832 | tf_op jit(solution)/shard_map/ppermute | solution.py:69
  32.3 8.7 %collective-permute-start.9 = (f32[128,384]{0,1:T(8,128)S(1)}, f32[128,384]{0,1:T(8,128)S(1)}, u32[]{:S(2)}, u32[]{:S(2)}) collective-permute-start(f32[128,384]{0,1:T(8,128)S(1)} %add_add_fusion.1), channel_id=1, source_target_pairs={{0,96},{2,98},{4,100},{6,102},{8,104},{10,106},{12,108},{14,110},{... | collective-permute-start | bytes 589832 | tf_op jit(solution)/shard_map/ppermute | solution.py:69
  33.9 8.2 %collective-permute-start.8 = (f32[128,384]{0,1:T(8,128)S(1)}, f32[128,384]{0,1:T(8,128)S(1)}, u32[]{:S(2)}, u32[]{:S(2)}) collective-permute-start(f32[128,384]{0,1:T(8,128)S(1)} %add_add_fusion.1), channel_id=1, source_target_pairs={{0,64},{2,66},{4,68},{6,70},{8,72},{10,74},{12,76},{14,78},{16,80}... | collective-permute-start | bytes 589832 | tf_op jit(solution)/shard_map/ppermute | solution.py:69
  34.9 8.4 %collective-permute-start.7 = (f32[128,384]{0,1:T(8,128)S(1)}, f32[128,384]{0,1:T(8,128)S(1)}, u32[]{:S(2)}, u32[]{:S(2)}) collective-permute-start(f32[128,384]{0,1:T(8,128)S(1)} %add_add_fusion.1), channel_id=1, source_target_pairs={{0,32},{2,34},{4,36},{6,38},{8,40},{10,42},{12,44},{14,46},{16,48}... | collective-permute-start | bytes 589832 | tf_op jit(solution)/shard_map/ppermute | solution.py:69
  55.5 1.2 copy-start.2
  55.7 1.3 %copy-start = (f32[8,128,256]{2,1,0:T(8,128)S(1)}, f32[8,128,256]{2,1,0:T(8,128)}, u32[]{:S(2)}) copy-start(f32[8,128,256]{2,1,0:T(8,128)} %param.5) | copy-start | bytes 3145732
  55.8 1.6 %copy-start.1 = (f32[8,128,256]{2,1,0:T(8,128)S(1)}, f32[8,128,256]{2,1,0:T(8,128)}, u32[]{:S(2)}) copy-start(f32[8,128,256]{2,1,0:T(8,128)} %param.4) | copy-start | bytes 3145732
  59.1 29.9 %copy-start.3 = (f32[8,128,128]{2,1,0:T(8,128)}, f32[8,128,128]{2,1,0:T(8,128)S(1)}, u32[]{:S(2)}) copy-start(f32[8,128,128]{2,1,0:T(8,128)S(1)} %get-tuple-element.16.refs_1_) | copy-start | bytes 1572868
  59.1 29.9 %copy-start.4 = (f32[8,128,128]{2,1,0:T(8,128)}, f32[8,128,128]{2,1,0:T(8,128)S(1)}, u32[]{:S(2)}) copy-start(f32[8,128,128]{2,1,0:T(8,128)S(1)} %get-tuple-element.15.mid_ref) | copy-start | bytes 1572868
  59.1 20.0 %collective-permute-start.15 = (f32[8,128,128]{2,1,0:T(8,128)S(1)}, f32[8,128,128]{2,1,0:T(8,128)S(1)}, u32[]{:S(2)}, u32[]{:S(2)}) collective-permute-start(f32[8,128,128]{2,1,0:T(8,128)S(1)} %get-tuple-element.15.mid_ref), channel_id=1, source_target_pairs={{2,0},{4,2},{6,4},{8,6},{10,8},{12,10},{14,12},{16,14},{18,16},{20... | collective-permute-start | bytes 1572872 | tf_op jit(solution)/shard_map/ppermute | solution.py:24
  67.0 19.2 %collective-permute-start.14 = (f32[8,128,128]{2,1,0:T(8,128)S(1)}, f32[8,128,128]{2,1,0:T(8,128)S(1)}, u32[]{:S(2)}, u32[]{:S(2)}) collective-permute-start(f32[8,128,128]{2,1,0:T(8,128)S(1)} %get-tuple-element.15.mid_ref), channel_id=1, source_target_pairs={{0,2},{2,4},{4,6},{6,8},{8,10},{10,12},{12,14},{14,16},{16,18},{18... | collective-permute-start | bytes 1572872 | tf_op jit(solution)/shard_map/ppermute | solution.py:24
  69.0 19.9 %collective-permute-start.11 = (f32[8,128,128]{2,1,0:T(8,128)S(1)}, f32[8,128,128]{2,1,0:T(8,128)S(1)}, u32[]{:S(2)}, u32[]{:S(2)}) collective-permute-start(f32[8,128,128]{2,1,0:T(8,128)S(1)} %get-tuple-element.16.refs_1_), channel_id=1, source_target_pairs={{2,0},{4,2},{6,4},{8,6},{10,8},{12,10},{14,12},{16,14},{18,16},{20... | collective-permute-start | bytes 1572872 | tf_op jit(solution)/shard_map/ppermute | solution.py:24
  77.1 18.7 %collective-permute-start.10 = (f32[8,128,128]{2,1,0:T(8,128)S(1)}, f32[8,128,128]{2,1,0:T(8,128)S(1)}, u32[]{:S(2)}, u32[]{:S(2)}) collective-permute-start(f32[8,128,128]{2,1,0:T(8,128)S(1)} %get-tuple-element.16.refs_1_), channel_id=1, source_target_pairs={{0,2},{2,4},{4,6},{6,8},{8,10},{10,12},{12,14},{14,16},{16,18},{18... | collective-permute-start | bytes 1572872 | tf_op jit(solution)/shard_map/ppermute | solution.py:24
  79.1 21.9 %copy-start.5 = (f32[8,128,128]{2,1,0:T(8,128)}, f32[8,128,128]{2,1,0:T(8,128)S(1)}, u32[]{:S(2)}) copy-start(f32[8,128,128]{2,1,0:T(8,128)S(1)} %collective-permute-done.15.down_ref) | copy-start | bytes 1572868
  86.3 10.4 %copy-start.8 = (f32[8,128,128]{2,1,0:T(8,128)}, f32[8,128,128]{2,1,0:T(8,128)S(1)}, u32[]{:S(2)}) copy-start(f32[8,128,128]{2,1,0:T(8,128)S(1)} %collective-permute-done.14.up_ref) | copy-start | bytes 1572868
  86.3 13.2 %collective-permute-start.16 = (f32[24,8,128]{2,1,0:T(8,128)S(1)}, f32[24,8,128]{2,1,0:T(8,128)S(1)}, u32[]{:S(2)}, u32[]{:S(2)}) collective-permute-start(f32[24,8,128]{2,1,0:T(8,128)S(1)} %pad_maximum_fusion.3), channel_id=1, source_target_pairs={{0,1},{2,3},{4,5},{6,7},{8,9},{10,11},{12,13},{14,15},{16,17},{18,... | collective-permute-start | bytes 294920 | tf_op jit(solution)/shard_map/ppermute | solution.py:24
  87.6 11.9 %collective-permute-start.17 = (f32[24,8,128]{2,1,0:T(8,128)S(1)}, f32[24,8,128]{2,1,0:T(8,128)S(1)}, u32[]{:S(2)}, u32[]{:S(2)}) collective-permute-start(f32[24,8,128]{2,1,0:T(8,128)S(1)} %pad_maximum_fusion.4), channel_id=1, source_target_pairs={{1,0},{3,2},{5,4},{7,6},{9,8},{11,10},{13,12},{15,14},{17,16},{19,... | collective-permute-start | bytes 294920 | tf_op jit(solution)/shard_map/ppermute | solution.py:24
  88.9 21.2 %copy-start.6 = (f32[8,128,128]{2,1,0:T(8,128)}, f32[8,128,128]{2,1,0:T(8,128)S(1)}, u32[]{:S(2)}) copy-start(f32[8,128,128]{2,1,0:T(8,128)S(1)} %collective-permute-done.11.refs_2_) | copy-start | bytes 1572868
  95.8 0.8 copy-start.7
  96.6 13.4 %collective-permute-start.12 = (f32[24,8,128]{2,1,0:T(8,128)S(1)}, f32[24,8,128]{2,1,0:T(8,128)S(1)}, u32[]{:S(2)}, u32[]{:S(2)}) collective-permute-start(f32[24,8,128]{2,1,0:T(8,128)S(1)} %pad_maximum_fusion.1), channel_id=1, source_target_pairs={{0,1},{2,3},{4,5},{6,7},{8,9},{10,11},{12,13},{14,15},{16,17},{18,... | collective-permute-start | bytes 294920 | tf_op jit(solution)/shard_map/ppermute | solution.py:24
  98.0 12.1 %collective-permute-start.13 = (f32[24,8,128]{2,1,0:T(8,128)S(1)}, f32[24,8,128]{2,1,0:T(8,128)S(1)}, u32[]{:S(2)}, u32[]{:S(2)}) collective-permute-start(f32[24,8,128]{2,1,0:T(8,128)S(1)} %pad_maximum_fusion.2), channel_id=1, source_target_pairs={{1,0},{3,2},{5,4},{7,6},{9,8},{11,10},{13,12},{15,14},{17,16},{19,... | collective-permute-start | bytes 294920 | tf_op jit(solution)/shard_map/ppermute | solution.py:24
  99.5 1.4 %copy-start.9 = (f32[24,8,128]{2,1,0:T(8,128)}, f32[24,8,128]{2,1,0:T(8,128)S(1)}, u32[]{:S(2)}) copy-start(f32[24,8,128]{2,1,0:T(8,128)S(1)} %collective-permute-done.16.left_ref) | copy-start | bytes 294916
  99.5 1.4 %copy-start.10 = (f32[24,8,128]{2,1,0:T(8,128)}, f32[24,8,128]{2,1,0:T(8,128)S(1)}, u32[]{:S(2)}) copy-start(f32[24,8,128]{2,1,0:T(8,128)S(1)} %collective-permute-done.17.right_ref) | copy-start | bytes 294916
  110.1 0.6 copy-start.11
  110.1 0.7 copy-start.12
where the time goes:
time: 122 us; the launch traced here: 120 us
  waiting for transfers between devices  39.4 us (32%)
  starting transfers between devices  38.8 us (32%)
  Pallas kernels  18.3 us (15%)
  matrix products  16 us (13%)
  local copies, waits for them, and re-layouts  3.87 us (3%)
  between operations  2.66 us (2%)
    ppermute x8, starting transfers between devices, shifted(): return lax.ppermute(x, axis, pairs)  25.3 us
    ppermute x9, waiting for transfers between devices, all_sum(): lax.ppermute(x, axis, [(i, i ^ k * step) for i in range(length)])  24 us
    pallas_call x2, Pallas kernels, tv_local(): pl.pallas_call(body, grid=(1,), in_specs=in_specs, out_specs=[pl.BlockSpe...  18.3 us
    dot_general x39, matrix products, matmul(): jnp.dot(left, right, precision=lax.Precision.HIGH, preferred_element_type...  16 us
    ppermute x8, waiting for transfers between devices, shifted(): return lax.ppermute(x, axis, pairs)  14 us
    ppermute x9, starting transfers between devices, all_sum(): lax.ppermute(x, axis, [(i, i ^ k * step) for i in range(length)])  13.4 us
  transfers between devices with their start and end apart: 18, of which 10 were waited for; matrix products, arithmetic and copies ran while one was open for 1% of the time, Pallas kernels for 8%

commit v1 on v0

--- a/solution.py
+++ b/solution.py
@@ -45,7 +45,13 @@
     return 0.5 * matmul(identity - cutoff * inverse, identity + signed)
 
 
-def halo_pieces(block):
+def halo_pieces(block, cols_first=False):
+    if cols_first:
+        left = shifted(block[:, -HALO:], "cols", 1)
+        right = shifted(block[:, :HALO], "cols", -1)
+        up = shifted(jnp.concatenate([left[-HALO:], block[-HALO:], right[-HALO:]], axis=1), "rows", 1)
+        down = shifted(jnp.concatenate([left[:HALO], block[:HALO], right[:HALO]], axis=1), "rows", -1)
+        return up, block, down, left, right
     up = shifted(block[-HALO:], "rows", 1)
     down = shifted(block[:HALO], "rows", -1)
     left = shifted(jnp.concatenate([up[:, -HALO:], block[:, -HALO:], down[:, -HALO:]], axis=0), "cols", 1)
@@ -83,9 +89,13 @@
     return jnp.concatenate([top, bottom], axis=0)
 
 
-def tv_kernel(up_ref, mid_ref, down_ref, left_ref, right_ref, kx_ref, ky_ref, fg_ref, dual_ref):
-    t = jnp.concatenate([up_ref[...], mid_ref[...], down_ref[...]], axis=0)
-    t = jnp.concatenate([left_ref[...], t, right_ref[...]], axis=1)
+def tv_kernel(up_ref, mid_ref, down_ref, left_ref, right_ref, kx_ref, ky_ref, fg_ref, dual_ref, cols_first=False):
+    if cols_first:
+        t = jnp.concatenate([left_ref[...], mid_ref[...], right_ref[...]], axis=1)
+        t = jnp.concatenate([up_ref[...], t, down_ref[...]], axis=0)
+    else:
+        t = jnp.concatenate([up_ref[...], mid_ref[...], down_ref[...]], axis=0)
+        t = jnp.concatenate([left_ref[...], t, right_ref[...]], axis=1)
     rows, cols = t.shape[0], t.shape[1]
     kx = kx_ref[...]
     ky = ky_ref[...][None]
@@ -137,7 +147,7 @@
         aliases = {7: 0, 8: 1}
 
         def body(*refs):
-            tv_kernel(*refs[:7], *refs[9:])
+            tv_kernel(*refs[:7], *refs[9:], cols_first=True)
 
     return pl.pallas_call(
         body,
@@ -176,7 +186,7 @@
     ky = jnp.broadcast_to(jnp.where(keep_y, 1.0, 0.0).astype(jnp.float32)[0], (ext_cols, lanes))
     outs = None
     for chunk in range(frames // lanes):
-        pieces = halo_pieces(target[:, :, chunk * lanes : (chunk + 1) * lanes])
+        pieces = halo_pieces(target[:, :, chunk * lanes : (chunk + 1) * lanes], cols_first=chunk > 0)
         outs = tv_local(pieces, kx, ky, chunk, frames, outs)
     new_foreground, new_dual = outs
     return (background, new_foreground, new_dual)

time: 122 us -> 114 us (0.934); the launches traced: 120 us -> 114 us
  waiting for transfers between devices: 39.4 us -> 31.6 us
  starting transfers between devices: 38.8 us -> 41.2 us
    ppermute x8, waiting for transfers between devices: 14 us -> 6.19 us  [shifted(): return lax.ppermute(x, axis, pairs)]
    ppermute x8, starting transfers between devices: 25.3 us -> 27.7 us  [shifted(): return lax.ppermute(x, axis, pairs)]
  transfers between devices with their start and end apart: 18 -> 18, of which waited for: 10 -> 11; matrix products, arithmetic and copies ran while one was open for 1% -> 1% of each run, Pallas kernels for 8% -> 8%
where the time goes in v1:
time: 114 us
  starting transfers between devices  41.2 us (36%)
  waiting for transfers between devices  31.6 us (28%)
  Pallas kernels  18.3 us (16%)
  matrix products  16 us (14%)
  local copies, waits for them, and re-layouts  2.93 us (3%)
  between operations  2.63 us (2%)
    ppermute x8, starting transfers between devices, shifted(): return lax.ppermute(x, axis, pairs)  27.7 us
    ppermute x9, waiting for transfers between devices, all_sum(): lax.ppermute(x, axis, [(i, i ^ k * step) for i in range(length)])  24 us
    pallas_call x2, Pallas kernels, tv_local(): pl.pallas_call(body, grid=(1,), in_specs=in_specs, out_specs=[pl.BlockSpe...  18.3 us
    dot_general x39, matrix products, matmul(): jnp.dot(left, right, precision=lax.Precision.HIGH, preferred_element_type...  16 us
    ppermute x9, starting transfers between devices, all_sum(): lax.ppermute(x, axis, [(i, i ^ k * step) for i in range(length)])  13.4 us
    ppermute x8, waiting for transfers between devices, shifted(): return lax.ppermute(x, axis, pairs)  6.19 us
  transfers between devices with their start and end apart: 18, of which 11 were waited for; matrix products, arithmetic and copies ran while one was open for 1% of the time, Pallas kernels for 8%

profile of v1, /device:TPU:8, one launch (start us, length us, event | category | flops | bytes accessed | tf_op | source)
XLA Modules:
  0.0 113.6 jit_solution(15132596824089700294)
XLA Ops:
  0.6 3.5 %convolution_bitcast_fusion = f32[256,256]{0,1:T(8,128)S(1)} fusion(f32[8,128,256]{2,1,0:T(8,128)} %param.5, f32[8,128,256]{2,1,0:T(8,128)} %param.4, bf16[8,128,256]{2,1,0:T(8,128)(2,1)} %param.3), kind=kOutput, calls=%fused_computation.35 | convolution fusion | flops 403439616 | bytes 2883584 | tf_op jit(solution)/shard_map/dot_general | solution.py:28
  4.3 1.4 %collective-permute-done = f32[128,384]{0,1:T(8,128)S(1)} collective-permute-done((f32[128,384]{0,1:T(8,128)S(1)}, f32[128,384]{0,1:T(8,128)S(1)}, u32[]{:S(2)}, u32[]{:S(2)}) %collective-permute-start) | collective-permute-done | bytes 196640 | tf_op jit(solution)/shard_map/ppermute | solution.py:78
  5.8 2.8 %collective-permute-start.3 = (f32[128,384]{0,1:T(8,128)S(1)}, f32[128,384]{0,1:T(8,128)S(1)}, u32[]{:S(2)}, u32[]{:S(2)}) collective-permute-start(f32[128,384]{0,1:T(8,128)S(1)} %fusion.36), channel_id=1, source_target_pairs={{0,6},{2,4},{4,2},{6,0},{8,14},{10,12},{12,10},{14,8},{16,22},{18,... | collective-permute-start | bytes 589832 | tf_op jit(solution)/shard_map/ppermute | solution.py:75
  8.6 0.8 collective-permute-start.2
  9.4 0.5 collective-permute-start.1
  9.9 8.3 %collective-permute-done.3 = f32[128,384]{0,1:T(8,128)S(1)} collective-permute-done((f32[128,384]{0,1:T(8,128)S(1)}, f32[128,384]{0,1:T(8,128)S(1)}, u32[]{:S(2)}, u32[]{:S(2)}) %collective-permute-start.3) | collective-permute-done | bytes 196640 | tf_op jit(solution)/shard_map/ppermute | solution.py:75
  18.2 0.6 collective-permute-done.1
  18.9 4.1 %collective-permute-start.6 = (f32[128,384]{0,1:T(8,128)S(1)}, f32[128,384]{0,1:T(8,128)S(1)}, u32[]{:S(2)}, u32[]{:S(2)}) collective-permute-start(f32[128,384]{0,1:T(8,128)S(1)} %add_add_fusion.2), channel_id=1, source_target_pairs={{0,24},{2,26},{4,28},{6,30},{8,16},{10,18},{12,20},{14,22},{16,8},... | collective-permute-start | bytes 589832 | tf_op jit(solution)/shard_map/ppermute | solution.py:75
  23.0 0.9 collective-permute-start.4
  24.0 6.6 %collective-permute-done.6 = f32[128,384]{0,1:T(8,128)S(1)} collective-permute-done((f32[128,384]{0,1:T(8,128)S(1)}, f32[128,384]{0,1:T(8,128)S(1)}, u32[]{:S(2)}, u32[]{:S(2)}) %collective-permute-start.6) | collective-permute-done | bytes 196640 | tf_op jit(solution)/shard_map/ppermute | solution.py:75
  30.6 1.6 %collective-permute-done.5 = f32[128,384]{0,1:T(8,128)S(1)} collective-permute-done((f32[128,384]{0,1:T(8,128)S(1)}, f32[128,384]{0,1:T(8,128)S(1)}, u32[]{:S(2)}, u32[]{:S(2)}) %collective-permute-start.5) | collective-permute-done | bytes 196640 | tf_op jit(solution)/shard_map/ppermute | solution.py:75
  32.3 1.7 %collective-permute-start.9 = (f32[128,384]{0,1:T(8,128)S(1)}, f32[128,384]{0,1:T(8,128)S(1)}, u32[]{:S(2)}, u32[]{:S(2)}) collective-permute-start(f32[128,384]{0,1:T(8,128)S(1)} %add_add_fusion.1), channel_id=1, source_target_pairs={{0,96},{2,98},{4,100},{6,102},{8,104},{10,106},{12,108},{14,110},{... | collective-permute-start | bytes 589832 | tf_op jit(solution)/shard_map/ppermute | solution.py:75
  33.9 0.9 collective-permute-start.8
  34.9 1.6 %collective-permute-start.7 = (f32[128,384]{0,1:T(8,128)S(1)}, f32[128,384]{0,1:T(8,128)S(1)}, u32[]{:S(2)}, u32[]{:S(2)}) collective-permute-start(f32[128,384]{0,1:T(8,128)S(1)} %add_add_fusion.1), channel_id=1, source_target_pairs={{0,32},{2,34},{4,36},{6,38},{8,40},{10,42},{12,44},{14,46},{16,48}... | collective-permute-start | bytes 589832 | tf_op jit(solution)/shard_map/ppermute | solution.py:75
  36.5 4.5 %collective-permute-done.9 = f32[128,384]{0,1:T(8,128)S(1)} collective-permute-done((f32[128,384]{0,1:T(8,128)S(1)}, f32[128,384]{0,1:T(8,128)S(1)}, u32[]{:S(2)}, u32[]{:S(2)}) %collective-permute-start.9) | collective-permute-done | bytes 196640 | tf_op jit(solution)/shard_map/ppermute | solution.py:75
  41.0 1.2 %collective-permute-done.8 = f32[128,384]{0,1:T(8,128)S(1)} collective-permute-done((f32[128,384]{0,1:T(8,128)S(1)}, f32[128,384]{0,1:T(8,128)S(1)}, u32[]{:S(2)}, u32[]{:S(2)}) %collective-permute-start.8) | collective-permute-done | bytes 196640 | tf_op jit(solution)/shard_map/ppermute | solution.py:75
  42.2 1.1 %collective-permute-done.7 = f32[128,384]{0,1:T(8,128)S(1)} collective-permute-done((f32[128,384]{0,1:T(8,128)S(1)}, f32[128,384]{0,1:T(8,128)S(1)}, u32[]{:S(2)}, u32[]{:S(2)}) %collective-permute-start.7) | collective-permute-done | bytes 196640 | tf_op jit(solution)/shard_map/ppermute | solution.py:75
  43.5 0.7 multiply_reduce_fusion
  44.8 0.3 fusion.15
  45.1 0.4 fusion.29
  45.8 0.3 fusion.14
  46.1 0.3 fusion.43
  46.3 0.3 fusion.42
  46.6 0.3 fusion.13
  46.9 0.3 fusion.45
  47.5 0.3 fusion.12
  47.7 0.3 fusion.47
  48.3 0.3 fusion.11
  48.6 0.3 fusion.49
  49.1 0.3 fusion.10
  50.0 0.3 fusion.9
  51.1 0.9 select_reduce_fusion
  52.9 0.3 fusion.20
  53.2 0.3 fusion.6
  53.5 0.3 fusion.54
  53.8 0.3 fusion.5
  54.0 0.3 fusion.55
  54.3 0.3 fusion.4
  54.6 0.3 fusion.56
  54.9 0.3 fusion.3
  55.2 0.3 fusion.57
  55.5 0.3 fusion.2
  55.8 0.3 fusion.58
  56.1 0.3 fusion.16
  56.3 0.3 fusion
  56.6 0.4 copy-done.1
  57.0 0.3 copy-done.2
  57.3 1.6 %fusion.18 = (f32[8,128,256]{2,1,0:T(8,128)S(1)}, f32[8,128,256]{2,1,0:T(8,128)}) fusion(f32[8,128,256]{2,1,0:T(8,128)S(1)} %copy-done.1, bf16[8,128,256]{2,1,0:T(8,128)(2,1)S(1)} %copy-done.3, f32[256,256,1]{1,0,2:T(8,128)S(1)} %fusion, f32[8,128,256]{2,1,0:T(8,128)S(1)} %copy-done.2), kind=kOutput, calls=%fused_computation.37 | convolution fusion | flops 404226048 | bytes 4980736 | tf_op jit(solution)/shard_map/dot_general | solution.py:28
  59.1 7.9 %collective-permute-start.15 = (f32[8,128,128]{2,1,0:T(8,128)S(1)}, f32[8,128,128]{2,1,0:T(8,128)S(1)}, u32[]{:S(2)}, u32[]{:S(2)}) collective-permute-start(f32[8,128,128]{2,1,0:T(8,128)S(1)} %get-tuple-element.15.mid_ref), channel_id=1, source_target_pairs={{2,0},{4,2},{6,4},{8,6},{10,8},{12,10},{14,12},{16,14},{18,16},{20... | collective-permute-start | bytes 1572872 | tf_op jit(solution)/shard_map/ppermute | solution.py:24
  67.0 1.9 %collective-permute-start.14 = (f32[8,128,128]{2,1,0:T(8,128)S(1)}, f32[8,128,128]{2,1,0:T(8,128)S(1)}, u32[]{:S(2)}, u32[]{:S(2)}) collective-permute-start(f32[8,128,128]{2,1,0:T(8,128)S(1)} %get-tuple-element.15.mid_ref), channel_id=1, source_target_pairs={{0,2},{2,4},{4,6},{6,8},{8,10},{10,12},{12,14},{14,16},{16,18},{18... | collective-permute-start | bytes 1572872 | tf_op jit(solution)/shard_map/ppermute | solution.py:24
  69.0 1.3 %collective-permute-start.11 = (f32[8,8,128]{2,1,0:T(8,128)S(1)}, f32[8,8,128]{2,1,0:T(8,128)S(1)}, u32[]{:S(2)}, u32[]{:S(2)}) collective-permute-start(f32[8,8,128]{2,1,0:T(8,128)S(1)} %get-tuple-element.13), channel_id=1, source_target_pairs={{1,0},{3,2},{5,4},{7,6},{9,8},{11,10},{13,12},{15,14},{17,16},{19,... | collective-permute-start | bytes 98312 | tf_op jit(solution)/shard_map/ppermute | solution.py:24
  70.3 3.0 %collective-permute-start.10 = (f32[8,8,128]{2,1,0:T(8,128)S(1)}, f32[8,8,128]{2,1,0:T(8,128)S(1)}, u32[]{:S(2)}, u32[]{:S(2)}) collective-permute-start(f32[8,8,128]{2,1,0:T(8,128)S(1)} %get-tuple-element.14), channel_id=1, source_target_pairs={{0,1},{2,3},{4,5},{6,7},{8,9},{10,11},{12,13},{14,15},{16,17},{18,... | collective-permute-start | bytes 98312 | tf_op jit(solution)/shard_map/ppermute | solution.py:24
  73.4 0.8 collective-permute-done.10.refs_3_
  74.2 0.5 copy-done.8
  74.8 8.1 %collective-permute-start.13 = (f32[8,144,128]{2,1,0:T(8,128)S(1)}, f32[8,144,128]{2,1,0:T(8,128)}, u32[]{:S(2)}, u32[]{:S(2)}) collective-permute-start(f32[8,144,128]{2,1,0:T(8,128)S(1)} %pad_maximum_fusion), channel_id=1, source_target_pairs={{2,0},{4,2},{6,4},{8,6},{10,8},{12,10},{14,12},{16,14},{18,16},{20... | collective-permute-start | bytes 1769480 | tf_op jit(solution)/shard_map/ppermute | solution.py:24
  82.9 1.9 %collective-permute-start.12 = (f32[8,144,128]{2,1,0:T(8,128)S(1)}, f32[8,144,128]{2,1,0:T(8,128)}, u32[]{:S(2)}, u32[]{:S(2)}) collective-permute-start(f32[8,144,128]{2,1,0:T(8,128)S(1)} %pad_maximum_fusion), channel_id=1, source_target_pairs={{0,2},{2,4},{4,6},{6,8},{8,10},{10,12},{12,14},{14,16},{16,18},{18... | collective-permute-start | bytes 1769480 | tf_op jit(solution)/shard_map/ppermute | solution.py:24
  84.9 2.0 %collective-permute-start.16 = (f32[24,8,128]{2,1,0:T(8,128)S(1)}, f32[24,8,128]{2,1,0:T(8,128)S(1)}, u32[]{:S(2)}, u32[]{:S(2)}) collective-permute-start(f32[24,8,128]{2,1,0:T(8,128)S(1)} %pad_maximum_fusion.2), channel_id=1, source_target_pairs={{0,1},{2,3},{4,5},{6,7},{8,9},{10,11},{12,13},{14,15},{16,17},{18,... | collective-permute-start | bytes 294920 | tf_op jit(solution)/shard_map/ppermute | solution.py:24
  86.9 1.5 %collective-permute-start.17 = (f32[24,8,128]{2,1,0:T(8,128)S(1)}, f32[24,8,128]{2,1,0:T(8,128)S(1)}, u32[]{:S(2)}, u32[]{:S(2)}) collective-permute-start(f32[24,8,128]{2,1,0:T(8,128)S(1)} %pad_maximum_fusion.3), channel_id=1, source_target_pairs={{1,0},{3,2},{5,4},{7,6},{9,8},{11,10},{13,12},{15,14},{17,16},{19,... | collective-permute-start | bytes 294920 | tf_op jit(solution)/shard_map/ppermute | solution.py:24
  88.5 1.6 %collective-permute-done.17.right_ref = f32[24,8,128]{2,1,0:T(8,128)S(1)} collective-permute-done((f32[24,8,128]{2,1,0:T(8,128)S(1)}, f32[24,8,128]{2,1,0:T(8,128)S(1)}, u32[]{:S(2)}, u32[]{:S(2)}) %collective-permute-start.17) | collective-permute-done | bytes 98336 | tf_op jit(solution)/shard_map/ppermute | solution.py:24
  90.1 0.7 broadcast_in_dim.30.kx_ref.refs_5_
  90.8 0.7 broadcast_in_dim.33.ky_ref.refs_6_
  91.5 9.1 %shard_map.58 = (f32[8,128,256]{2,1,0:T(8,128)}, f32[8,128,256]{2,1,0:T(8,128)}) custom-call(f32[8,128,128]{2,1,0:T(8,128)} %copy-done.6, f32[8,128,128]{2,1,0:T(8,128)} %copy-done.4, f32[8,128,128]{2,1,0:T(8,128)} %copy-done.5, f32[24,8,128]{2,1,0:T(8,128)} %copy-done.9, f32[24,8,128]{2,1,0:T(8,128)} %copy-done.10, ...), custom_call_target="tpu_custom_call" | custom-call | tf_op jit(solution)/shard_map/pallas_call | solution.py:152
  100.7 3.7 %collective-permute-done.12.refs_0_ = f32[8,144,128]{2,1,0:T(8,128)} collective-permute-done((f32[8,144,128]{2,1,0:T(8,128)S(1)}, f32[8,144,128]{2,1,0:T(8,128)}, u32[]{:S(2)}, u32[]{:S(2)}) %collective-permute-start.12) | collective-permute-done | bytes 589856 | tf_op jit(solution)/shard_map/ppermute | solution.py:24
  104.4 9.2 %shard_map.59 = (f32[8,128,256]{2,1,0:T(8,128)}, f32[8,128,256]{2,1,0:T(8,128)}) custom-call(f32[8,144,128]{2,1,0:T(8,128)} %collective-permute-done.12.refs_0_, f32[8,128,128]{2,1,0:T(8,128)} %copy-done, f32[8,144,128]{2,1,0:T(8,128)} %collective-permute-done.13.refs_2_, f32[8,8,128]{2,1,0:T(8,128)} %copy-done.8, ...), custom_call_target="tpu_custom_call", output_to_operand_aliasing={{0}: (7, {}), {1}: (8, {})} | custom-call | tf_op jit(solution)/shard_map/pallas_call | solution.py:152
  (57 shorter events, 3.3 us)
Async XLA Ops:
  4.2 1.5 %collective-permute-start = (f32[128,384]{0,1:T(8,128)S(1)}, f32[128,384]{0,1:T(8,128)S(1)}, u32[]{:S(2)}, u32[]{:S(2)}) collective-permute-start(f32[128,384]{0,1:T(8,128)S(1)} %pad_maximum_fusion.1), channel_id=1, source_target_pairs={{0,1},{1,0},{2,3},{3,2},{4,5},{5,4},{6,7},{7,6},{8,9},{9,8},{10,11... | collective-permute-start | bytes 589832 | tf_op jit(solution)/shard_map/ppermute | solution.py:78
  5.8 12.4 %collective-permute-start.3 = (f32[128,384]{0,1:T(8,128)S(1)}, f32[128,384]{0,1:T(8,128)S(1)}, u32[]{:S(2)}, u32[]{:S(2)}) collective-permute-start(f32[128,384]{0,1:T(8,128)S(1)} %fusion.36), channel_id=1, source_target_pairs={{0,6},{2,4},{4,2},{6,0},{8,14},{10,12},{12,10},{14,8},{16,22},{18,... | collective-permute-start | bytes 589832 | tf_op jit(solution)/shard_map/ppermute | solution.py:75
  8.6 9.6 %collective-permute-start.2 = (f32[128,384]{0,1:T(8,128)S(1)}, f32[128,384]{0,1:T(8,128)S(1)}, u32[]{:S(2)}, u32[]{:S(2)}) collective-permute-start(f32[128,384]{0,1:T(8,128)S(1)} %fusion.36), channel_id=1, source_target_pairs={{0,4},{2,6},{4,0},{6,2},{8,12},{10,14},{12,8},{14,10},{16,20},{18,... | collective-permute-start | bytes 589832 | tf_op jit(solution)/shard_map/ppermute | solution.py:75
  9.4 9.4 %collective-permute-start.1 = (f32[128,384]{0,1:T(8,128)S(1)}, f32[128,384]{0,1:T(8,128)S(1)}, u32[]{:S(2)}, u32[]{:S(2)}) collective-permute-start(f32[128,384]{0,1:T(8,128)S(1)} %fusion.36), channel_id=1, source_target_pairs={{0,2},{2,0},{4,6},{6,4},{8,10},{10,8},{12,14},{14,12},{16,18},{18,... | collective-permute-start | bytes 589832 | tf_op jit(solution)/shard_map/ppermute | solution.py:75
  18.9 11.7 %collective-permute-start.6 = (f32[128,384]{0,1:T(8,128)S(1)}, f32[128,384]{0,1:T(8,128)S(1)}, u32[]{:S(2)}, u32[]{:S(2)}) collective-permute-start(f32[128,384]{0,1:T(8,128)S(1)} %add_add_fusion.2), channel_id=1, source_target_pairs={{0,24},{2,26},{4,28},{6,30},{8,16},{10,18},{12,20},{14,22},{16,8},... | collective-permute-start | bytes 589832 | tf_op jit(solution)/shard_map/ppermute | solution.py:75
  23.0 9.2 %collective-permute-start.5 = (f32[128,384]{0,1:T(8,128)S(1)}, f32[128,384]{0,1:T(8,128)S(1)}, u32[]{:S(2)}, u32[]{:S(2)}) collective-permute-start(f32[128,384]{0,1:T(8,128)S(1)} %add_add_fusion.2), channel_id=1, source_target_pairs={{0,16},{2,18},{4,20},{6,22},{8,24},{10,26},{12,28},{14,30},{16,0},... | collective-permute-start | bytes 589832 | tf_op jit(solution)/shard_map/ppermute | solution.py:75
  23.0 9.2 %collective-permute-start.4 = (f32[128,384]{0,1:T(8,128)S(1)}, f32[128,384]{0,1:T(8,128)S(1)}, u32[]{:S(2)}, u32[]{:S(2)}) collective-permute-start(f32[128,384]{0,1:T(8,128)S(1)} %add_add_fusion.2), channel_id=1, source_target_pairs={{0,8},{2,10},{4,12},{6,14},{8,0},{10,2},{12,4},{14,6},{16,24},{18,... | collective-permute-start | bytes 589832 | tf_op jit(solution)/shard_map/ppermute | solution.py:75
  32.3 8.7 %collective-permute-start.9 = (f32[128,384]{0,1:T(8,128)S(1)}, f32[128,384]{0,1:T(8,128)S(1)}, u32[]{:S(2)}, u32[]{:S(2)}) collective-permute-start(f32[128,384]{0,1:T(8,128)S(1)} %add_add_fusion.1), channel_id=1, source_target_pairs={{0,96},{2,98},{4,100},{6,102},{8,104},{10,106},{12,108},{14,110},{... | collective-permute-start | bytes 589832 | tf_op jit(solution)/shard_map/ppermute | solution.py:75
  33.9 8.2 %collective-permute-start.8 = (f32[128,384]{0,1:T(8,128)S(1)}, f32[128,384]{0,1:T(8,128)S(1)}, u32[]{:S(2)}, u32[]{:S(2)}) collective-permute-start(f32[128,384]{0,1:T(8,128)S(1)} %add_add_fusion.1), channel_id=1, source_target_pairs={{0,64},{2,66},{4,68},{6,70},{8,72},{10,74},{12,76},{14,78},{16,80}... | collective-permute-start | bytes 589832 | tf_op jit(solution)/shard_map/ppermute | solution.py:75
  34.9 8.4 %collective-permute-start.7 = (f32[128,384]{0,1:T(8,128)S(1)}, f32[128,384]{0,1:T(8,128)S(1)}, u32[]{:S(2)}, u32[]{:S(2)}) collective-permute-start(f32[128,384]{0,1:T(8,128)S(1)} %add_add_fusion.1), channel_id=1, source_target_pairs={{0,32},{2,34},{4,36},{6,38},{8,40},{10,42},{12,44},{14,46},{16,48}... | collective-permute-start | bytes 589832 | tf_op jit(solution)/shard_map/ppermute | solution.py:75
  55.5 1.2 %copy-start.3 = (bf16[8,128,256]{2,1,0:T(8,128)(2,1)S(1)}, bf16[8,128,256]{2,1,0:T(8,128)(2,1)}, u32[]{:S(2)}) copy-start(bf16[8,128,256]{2,1,0:T(8,128)(2,1)} %param.3) | copy-start | bytes 1572868
  55.7 1.3 %copy-start.1 = (f32[8,128,256]{2,1,0:T(8,128)S(1)}, f32[8,128,256]{2,1,0:T(8,128)}, u32[]{:S(2)}) copy-start(f32[8,128,256]{2,1,0:T(8,128)} %param.5) | copy-start | bytes 3145732
  55.8 1.6 %copy-start.2 = (f32[8,128,256]{2,1,0:T(8,128)S(1)}, f32[8,128,256]{2,1,0:T(8,128)}, u32[]{:S(2)}) copy-start(f32[8,128,256]{2,1,0:T(8,128)} %param.4) | copy-start | bytes 3145732
  59.1 15.1 %copy-start = (f32[8,128,128]{2,1,0:T(8,128)}, f32[8,128,128]{2,1,0:T(8,128)S(1)}, u32[]{:S(2)}) copy-start(f32[8,128,128]{2,1,0:T(8,128)S(1)} %get-tuple-element.16.refs_1_) | copy-start | bytes 1572868
  59.1 15.1 %copy-start.4 = (f32[8,128,128]{2,1,0:T(8,128)}, f32[8,128,128]{2,1,0:T(8,128)S(1)}, u32[]{:S(2)}) copy-start(f32[8,128,128]{2,1,0:T(8,128)S(1)} %get-tuple-element.15.mid_ref) | copy-start | bytes 1572868
  59.1 25.8 %collective-permute-start.15 = (f32[8,128,128]{2,1,0:T(8,128)S(1)}, f32[8,128,128]{2,1,0:T(8,128)S(1)}, u32[]{:S(2)}, u32[]{:S(2)}) collective-permute-start(f32[8,128,128]{2,1,0:T(8,128)S(1)} %get-tuple-element.15.mid_ref), channel_id=1, source_target_pairs={{2,0},{4,2},{6,4},{8,6},{10,8},{12,10},{14,12},{16,14},{18,16},{20... | collective-permute-start | bytes 1572872 | tf_op jit(solution)/shard_map/ppermute | solution.py:24
  67.0 17.8 %collective-permute-start.14 = (f32[8,128,128]{2,1,0:T(8,128)S(1)}, f32[8,128,128]{2,1,0:T(8,128)S(1)}, u32[]{:S(2)}, u32[]{:S(2)}) collective-permute-start(f32[8,128,128]{2,1,0:T(8,128)S(1)} %get-tuple-element.15.mid_ref), channel_id=1, source_target_pairs={{0,2},{2,4},{4,6},{6,8},{8,10},{10,12},{12,14},{14,16},{16,18},{18... | collective-permute-start | bytes 1572872 | tf_op jit(solution)/shard_map/ppermute | solution.py:24
  69.0 4.4 %collective-permute-start.11 = (f32[8,8,128]{2,1,0:T(8,128)S(1)}, f32[8,8,128]{2,1,0:T(8,128)S(1)}, u32[]{:S(2)}, u32[]{:S(2)}) collective-permute-start(f32[8,8,128]{2,1,0:T(8,128)S(1)} %get-tuple-element.13), channel_id=1, source_target_pairs={{1,0},{3,2},{5,4},{7,6},{9,8},{11,10},{13,12},{15,14},{17,16},{19,... | collective-permute-start | bytes 98312 | tf_op jit(solution)/shard_map/ppermute | solution.py:24
  70.3 3.9 %collective-permute-start.10 = (f32[8,8,128]{2,1,0:T(8,128)S(1)}, f32[8,8,128]{2,1,0:T(8,128)S(1)}, u32[]{:S(2)}, u32[]{:S(2)}) collective-permute-start(f32[8,8,128]{2,1,0:T(8,128)S(1)} %get-tuple-element.14), channel_id=1, source_target_pairs={{0,1},{2,3},{4,5},{6,7},{8,9},{10,11},{12,13},{14,15},{16,17},{18,... | collective-permute-start | bytes 98312 | tf_op jit(solution)/shard_map/ppermute | solution.py:24
  73.3 0.9 copy-start.7
  74.2 0.6 copy-start.8
  74.8 25.9 %collective-permute-start.13 = (f32[8,144,128]{2,1,0:T(8,128)S(1)}, f32[8,144,128]{2,1,0:T(8,128)}, u32[]{:S(2)}, u32[]{:S(2)}) collective-permute-start(f32[8,144,128]{2,1,0:T(8,128)S(1)} %pad_maximum_fusion), channel_id=1, source_target_pairs={{2,0},{4,2},{6,4},{8,6},{10,8},{12,10},{14,12},{16,14},{18,16},{20... | collective-permute-start | bytes 1769480 | tf_op jit(solution)/shard_map/ppermute | solution.py:24
  82.9 21.5 %collective-permute-start.12 = (f32[8,144,128]{2,1,0:T(8,128)S(1)}, f32[8,144,128]{2,1,0:T(8,128)}, u32[]{:S(2)}, u32[]{:S(2)}) collective-permute-start(f32[8,144,128]{2,1,0:T(8,128)S(1)} %pad_maximum_fusion), channel_id=1, source_target_pairs={{0,2},{2,4},{4,6},{6,8},{8,10},{10,12},{12,14},{14,16},{16,18},{18... | collective-permute-start | bytes 1769480 | tf_op jit(solution)/shard_map/ppermute | solution.py:24
  84.8 6.7 %copy-start.5 = (f32[8,128,128]{2,1,0:T(8,128)}, f32[8,128,128]{2,1,0:T(8,128)S(1)}, u32[]{:S(2)}) copy-start(f32[8,128,128]{2,1,0:T(8,128)S(1)} %collective-permute-done.15.down_ref) | copy-start | bytes 1572868
  84.9 6.7 %copy-start.6 = (f32[8,128,128]{2,1,0:T(8,128)}, f32[8,128,128]{2,1,0:T(8,128)S(1)}, u32[]{:S(2)}) copy-start(f32[8,128,128]{2,1,0:T(8,128)S(1)} %collective-permute-done.14.up_ref) | copy-start | bytes 1572868
  84.9 3.5 %collective-permute-start.16 = (f32[24,8,128]{2,1,0:T(8,128)S(1)}, f32[24,8,128]{2,1,0:T(8,128)S(1)}, u32[]{:S(2)}, u32[]{:S(2)}) collective-permute-start(f32[24,8,128]{2,1,0:T(8,128)S(1)} %pad_maximum_fusion.2), channel_id=1, source_target_pairs={{0,1},{2,3},{4,5},{6,7},{8,9},{10,11},{12,13},{14,15},{16,17},{18,... | collective-permute-start | bytes 294920 | tf_op jit(solution)/shard_map/ppermute | solution.py:24
  86.9 3.2 %collective-permute-start.17 = (f32[24,8,128]{2,1,0:T(8,128)S(1)}, f32[24,8,128]{2,1,0:T(8,128)S(1)}, u32[]{:S(2)}, u32[]{:S(2)}) collective-permute-start(f32[24,8,128]{2,1,0:T(8,128)S(1)} %pad_maximum_fusion.3), channel_id=1, source_target_pairs={{1,0},{3,2},{5,4},{7,6},{9,8},{11,10},{13,12},{15,14},{17,16},{19,... | collective-permute-start | bytes 294920 | tf_op jit(solution)/shard_map/ppermute | solution.py:24
  88.5 3.1 %copy-start.9 = (f32[24,8,128]{2,1,0:T(8,128)}, f32[24,8,128]{2,1,0:T(8,128)S(1)}, u32[]{:S(2)}) copy-start(f32[24,8,128]{2,1,0:T(8,128)S(1)} %collective-permute-done.16.left_ref) | copy-start | bytes 294916
  90.1 1.4 %copy-start.10 = (f32[24,8,128]{2,1,0:T(8,128)}, f32[24,8,128]{2,1,0:T(8,128)S(1)}, u32[]{:S(2)}) copy-start(f32[24,8,128]{2,1,0:T(8,128)S(1)} %collective-permute-done.17.right_ref) | copy-start | bytes 294916

commit v2 on v1

--- a/solution.py
+++ b/solution.py
@@ -81,12 +81,15 @@
 
 def summed_gram(flat):
     local = matmul(flat.T, flat)
-    half = local.shape[0] // 2
-    packed = all_sum(jnp.concatenate([local[:half], local[half:, half:]], axis=1))
-    top = packed[:, : 2 * half]
-    corner = packed[:, 2 * half :]
-    bottom = jnp.concatenate([top[:, half:].T, corner], axis=1)
-    return jnp.concatenate([top, bottom], axis=0)
+    size = local.shape[0]
+    block = 32 if size % 32 == 0 else size
+    n = size // block
+    upper = [(i, j) for i in range(n) for j in range(i, n)]
+    packed = jnp.concatenate([local[i * block : (i + 1) * block, j * block : (j + 1) * block] for i, j in upper], axis=1)
+    packed = all_sum(packed)
+    piece = {ij: packed[:, k * block : (k + 1) * block] for k, ij in enumerate(upper)}
+    rows = [jnp.concatenate([piece[(i, j)] if i <= j else piece[(j, i)].T for j in range(n)], axis=1) for i in range(n)]
+    return jnp.concatenate(rows, axis=0)
 
 
 def tv_kernel(up_ref, mid_ref, down_ref, left_ref, right_ref, kx_ref, ky_ref, fg_ref, dual_ref, cols_first=False):

time: 114 us -> 113 us (level)
  waiting for transfers between devices: 31.6 us -> 25.6 us
  local copies, waits for them, and re-layouts: 2.93 us -> 7.98 us
    ppermute x9, waiting for transfers between devices: 24 us -> 18.2 us  [all_sum(): lax.ppermute(x, axis, [(i, i ^ k * step) for i in range(length)])]
    unnamed x23 -> x58, local copies, waits for them, and re-layouts: 1.36 us -> 4.32 us
    slice x4 -> x17, local copies, waits for them, and re-layouts: 0.04 us -> 1.66 us  [the longest x9 1.21 us: summed_gram(): packed[:, k * block:(k + 1) * block]]
where the time goes in v2:
time: 113 us
  starting transfers between devices  41.3 us (37%)
  waiting for transfers between devices  25.6 us (23%)
  Pallas kernels  18.3 us (16%)
  matrix products  15.9 us (14%)
  local copies, waits for them, and re-layouts  7.98 us (7%)
  between operations  2.76 us (2%)
    ppermute x8, starting transfers between devices, shifted(): return lax.ppermute(x, axis, pairs)  27.8 us
    pallas_call x2, Pallas kernels, tv_local(): pl.pallas_call(body, grid=(1,), in_specs=in_specs, out_specs=[pl.BlockSpe...  18.3 us
    ppermute x9, waiting for transfers between devices, all_sum(): lax.ppermute(x, axis, [(i, i ^ k * step) for i in range(length)])  18.2 us
    dot_general x39, matrix products, matmul(): jnp.dot(left, right, precision=lax.Precision.HIGH, preferred_element_type...  15.9 us
    ppermute x9, starting transfers between devices, all_sum(): lax.ppermute(x, axis, [(i, i ^ k * step) for i in range(length)])  13.4 us
    ppermute x8, waiting for transfers between devices, shifted(): return lax.ppermute(x, axis, pairs)  6.09 us
    unnamed x58, local copies, waits for them, and re-layouts  4.32 us
  transfers between devices with their start and end apart: 18, of which 11 were waited for; matrix products, arithmetic and copies ran while one was open for 1% of the time, Pallas kernels for 8%

profile of v2, /device:TPU:8, one launch (start us, length us, event | category | flops | bytes accessed | tf_op | source)
XLA Modules:
  0.0 112.9 jit_solution(11342535467760534913)
XLA Ops:
  0.6 3.6 %convolution_bitcast_fusion = f32[256,256]{1,0:T(8,128)S(1)} fusion(f32[8,128,256]{2,1,0:T(8,128)} %param.5, f32[8,128,256]{2,1,0:T(8,128)} %param.4, bf16[8,128,256]{2,1,0:T(8,128)(2,1)} %param.3), kind=kOutput, calls=%fused_computation.35 | convolution fusion | flops 403439616 | bytes 2883584 | tf_op jit(solution)/shard_map/dot_general | solution.py:28
  4.9 1.4 %collective-permute-done = f32[32,1152]{1,0:T(8,128)S(1)} collective-permute-done((f32[32,1152]{1,0:T(8,128)S(1)}, f32[32,1152]{1,0:T(8,128)S(1)}, u32[]{:S(2)}, u32[]{:S(2)}) %collective-permute-start) | collective-permute-done | bytes 147488 | tf_op jit(solution)/shard_map/ppermute | solution.py:78
  6.3 2.8 %collective-permute-start.3 = (f32[32,1152]{1,0:T(8,128)S(1)}, f32[32,1152]{1,0:T(8,128)S(1)}, u32[]{:S(2)}, u32[]{:S(2)}) collective-permute-start(f32[32,1152]{1,0:T(8,128)S(1)} %add.65), channel_id=1, source_target_pairs={{0,6},{2,4},{4,2},{6,0},{8,14},{10,12},{12,10},{14,8},{16,22},{18,... | collective-permute-start | bytes 442376 | tf_op jit(solution)/shard_map/ppermute | solution.py:75
  9.1 0.8 collective-permute-start.2
  9.9 0.5 collective-permute-start.1
  10.4 5.5 %collective-permute-done.3 = f32[32,1152]{1,0:T(8,128)S(1)} collective-permute-done((f32[32,1152]{1,0:T(8,128)S(1)}, f32[32,1152]{1,0:T(8,128)S(1)}, u32[]{:S(2)}, u32[]{:S(2)}) %collective-permute-start.3) | collective-permute-done | bytes 147488 | tf_op jit(solution)/shard_map/ppermute | solution.py:75
  15.9 1.4 %collective-permute-done.2 = f32[32,1152]{1,0:T(8,128)S(1)} collective-permute-done((f32[32,1152]{1,0:T(8,128)S(1)}, f32[32,1152]{1,0:T(8,128)S(1)}, u32[]{:S(2)}, u32[]{:S(2)}) %collective-permute-start.2) | collective-permute-done | bytes 147488 | tf_op jit(solution)/shard_map/ppermute | solution.py:75
  17.4 4.1 %collective-permute-start.6 = (f32[32,1152]{1,0:T(8,128)S(1)}, f32[32,1152]{1,0:T(8,128)S(1)}, u32[]{:S(2)}, u32[]{:S(2)}) collective-permute-start(f32[32,1152]{1,0:T(8,128)S(1)} %add_add_fusion.2), channel_id=1, source_target_pairs={{0,24},{2,26},{4,28},{6,30},{8,16},{10,18},{12,20},{14,22},{16,8},... | collective-permute-start | bytes 442376 | tf_op jit(solution)/shard_map/ppermute | solution.py:75
  21.5 0.9 collective-permute-start.4
  22.4 4.5 %collective-permute-done.6 = f32[32,1152]{1,0:T(8,128)S(1)} collective-permute-done((f32[32,1152]{1,0:T(8,128)S(1)}, f32[32,1152]{1,0:T(8,128)S(1)}, u32[]{:S(2)}, u32[]{:S(2)}) %collective-permute-start.6) | collective-permute-done | bytes 147488 | tf_op jit(solution)/shard_map/ppermute | solution.py:75
  26.9 2.1 %collective-permute-done.5 = f32[32,1152]{1,0:T(8,128)S(1)} collective-permute-done((f32[32,1152]{1,0:T(8,128)S(1)}, f32[32,1152]{1,0:T(8,128)S(1)}, u32[]{:S(2)}, u32[]{:S(2)}) %collective-permute-start.5) | collective-permute-done | bytes 147488 | tf_op jit(solution)/shard_map/ppermute | solution.py:75
  29.1 1.7 %collective-permute-start.9 = (f32[32,1152]{1,0:T(8,128)S(1)}, f32[32,1152]{1,0:T(8,128)S(1)}, u32[]{:S(2)}, u32[]{:S(2)}) collective-permute-start(f32[32,1152]{1,0:T(8,128)S(1)} %add_add_fusion.1), channel_id=1, source_target_pairs={{0,96},{2,98},{4,100},{6,102},{8,104},{10,106},{12,108},{14,110},{... | collective-permute-start | bytes 442376 | tf_op jit(solution)/shard_map/ppermute | solution.py:75
  30.7 0.9 collective-permute-start.8
  31.7 1.6 %collective-permute-start.7 = (f32[32,1152]{1,0:T(8,128)S(1)}, f32[32,1152]{1,0:T(8,128)S(1)}, u32[]{:S(2)}, u32[]{:S(2)}) collective-permute-start(f32[32,1152]{1,0:T(8,128)S(1)} %add_add_fusion.1), channel_id=1, source_target_pairs={{0,32},{2,34},{4,36},{6,38},{8,40},{10,42},{12,44},{14,46},{16,48}... | collective-permute-start | bytes 442376 | tf_op jit(solution)/shard_map/ppermute | solution.py:75
  33.3 1.8 %collective-permute-done.9 = f32[32,1152]{1,0:T(8,128)S(1)} collective-permute-done((f32[32,1152]{1,0:T(8,128)S(1)}, f32[32,1152]{1,0:T(8,128)S(1)}, u32[]{:S(2)}, u32[]{:S(2)}) %collective-permute-start.9) | collective-permute-done | bytes 147488 | tf_op jit(solution)/shard_map/ppermute | solution.py:75
  35.0 2.4 %collective-permute-done.8 = f32[32,1152]{1,0:T(8,128)S(1)} collective-permute-done((f32[32,1152]{1,0:T(8,128)S(1)}, f32[32,1152]{1,0:T(8,128)S(1)}, u32[]{:S(2)}, u32[]{:S(2)}) %collective-permute-start.8) | collective-permute-done | bytes 147488 | tf_op jit(solution)/shard_map/ppermute | solution.py:75
  37.4 0.6 collective-permute-done.7
  40.9 0.6 slice-done
  42.2 0.7 multiply_reduce_fusion
  43.8 0.3 fusion.28
  44.3 0.3 fusion.14
  45.2 0.3 fusion.13
  46.0 0.3 fusion.12
  46.9 0.3 fusion.11
  47.1 0.3 fusion.44
  47.7 0.3 fusion.10
  48.0 0.3 fusion.46
  48.5 0.3 fusion.9
  48.8 0.3 fusion.48
  49.4 0.3 fusion.8
  49.6 0.9 select_reduce_fusion
  51.5 0.3 fusion.20
  51.7 0.3 fusion.6
  52.0 0.3 fusion.49
  52.3 0.3 fusion.5
  52.6 0.3 fusion.50
  52.9 0.3 fusion.4
  53.2 0.3 fusion.51
  53.4 0.3 fusion.3
  53.7 0.3 fusion.52
  54.0 0.3 fusion.2
  54.3 0.3 fusion.53
  54.6 0.3 fusion.16
  54.9 0.3 fusion
  55.2 0.4 copy-done.2
  55.6 0.3 copy-done.3
  55.9 1.6 %fusion.18 = (f32[8,128,256]{2,1,0:T(8,128)S(1)}, f32[8,128,256]{2,1,0:T(8,128)}) fusion(f32[8,128,256]{2,1,0:T(8,128)S(1)} %copy-done.2, bf16[8,128,256]{2,1,0:T(8,128)(2,1)S(1)} %copy-done.4, f32[256,256,1]{1,0,2:T(8,128)S(1)} %fusion, f32[8,128,256]{2,1,0:T(8,128)S(1)} %copy-done.3), kind=kOutput, calls=%fused_computation.37 | convolution fusion | flops 404226048 | bytes 4980736 | tf_op jit(solution)/shard_map/dot_general | solution.py:28
  57.6 8.0 %collective-permute-start.15 = (f32[8,128,128]{2,1,0:T(8,128)S(1)}, f32[8,128,128]{2,1,0:T(8,128)S(1)}, u32[]{:S(2)}, u32[]{:S(2)}) collective-permute-start(f32[8,128,128]{2,1,0:T(8,128)S(1)} %get-tuple-element.15.mid_ref), channel_id=1, source_target_pairs={{2,0},{4,2},{6,4},{8,6},{10,8},{12,10},{14,12},{16,14},{18,16},{20... | collective-permute-start | bytes 1572872 | tf_op jit(solution)/shard_map/ppermute | solution.py:24
  65.6 1.9 %collective-permute-start.14 = (f32[8,128,128]{2,1,0:T(8,128)S(1)}, f32[8,128,128]{2,1,0:T(8,128)S(1)}, u32[]{:S(2)}, u32[]{:S(2)}) collective-permute-start(f32[8,128,128]{2,1,0:T(8,128)S(1)} %get-tuple-element.15.mid_ref), channel_id=1, source_target_pairs={{0,2},{2,4},{4,6},{6,8},{8,10},{10,12},{12,14},{14,16},{16,18},{18... | collective-permute-start | bytes 1572872 | tf_op jit(solution)/shard_map/ppermute | solution.py:24
  67.6 1.3 %collective-permute-start.11 = (f32[8,8,128]{2,1,0:T(8,128)S(1)}, f32[8,8,128]{2,1,0:T(8,128)S(1)}, u32[]{:S(2)}, u32[]{:S(2)}) collective-permute-start(f32[8,8,128]{2,1,0:T(8,128)S(1)} %get-tuple-element.13), channel_id=1, source_target_pairs={{1,0},{3,2},{5,4},{7,6},{9,8},{11,10},{13,12},{15,14},{17,16},{19,... | collective-permute-start | bytes 98312 | tf_op jit(solution)/shard_map/ppermute | solution.py:24
  68.9 3.0 %collective-permute-start.10 = (f32[8,8,128]{2,1,0:T(8,128)S(1)}, f32[8,8,128]{2,1,0:T(8,128)S(1)}, u32[]{:S(2)}, u32[]{:S(2)}) collective-permute-start(f32[8,8,128]{2,1,0:T(8,128)S(1)} %get-tuple-element.14), channel_id=1, source_target_pairs={{0,1},{2,3},{4,5},{6,7},{8,9},{10,11},{12,13},{14,15},{16,17},{18,... | collective-permute-start | bytes 98312 | tf_op jit(solution)/shard_map/ppermute | solution.py:24
  72.0 0.8 collective-permute-done.10.refs_3_
  72.8 0.5 copy-done.10
  73.4 8.1 %collective-permute-start.13 = (f32[8,144,128]{2,1,0:T(8,128)S(1)}, f32[8,144,128]{2,1,0:T(8,128)}, u32[]{:S(2)}, u32[]{:S(2)}) collective-permute-start(f32[8,144,128]{2,1,0:T(8,128)S(1)} %pad_maximum_fusion), channel_id=1, source_target_pairs={{2,0},{4,2},{6,4},{8,6},{10,8},{12,10},{14,12},{16,14},{18,16},{20... | collective-permute-start | bytes 1769480 | tf_op jit(solution)/shard_map/ppermute | solution.py:24
  81.5 1.9 %collective-permute-start.12 = (f32[8,144,128]{2,1,0:T(8,128)S(1)}, f32[8,144,128]{2,1,0:T(8,128)S(1)}, u32[]{:S(2)}, u32[]{:S(2)}) collective-permute-start(f32[8,144,128]{2,1,0:T(8,128)S(1)} %pad_maximum_fusion), channel_id=1, source_target_pairs={{0,2},{2,4},{4,6},{6,8},{8,10},{10,12},{12,14},{14,16},{16,18},{18... | collective-permute-start | bytes 1769480 | tf_op jit(solution)/shard_map/ppermute | solution.py:24
  83.5 2.0 %collective-permute-start.16 = (f32[24,8,128]{2,1,0:T(8,128)S(1)}, f32[24,8,128]{2,1,0:T(8,128)S(1)}, u32[]{:S(2)}, u32[]{:S(2)}) collective-permute-start(f32[24,8,128]{2,1,0:T(8,128)S(1)} %pad_maximum_fusion.1), channel_id=1, source_target_pairs={{0,1},{2,3},{4,5},{6,7},{8,9},{10,11},{12,13},{14,15},{16,17},{18,... | collective-permute-start | bytes 294920 | tf_op jit(solution)/shard_map/ppermute | solution.py:24
  85.5 1.5 %collective-permute-start.17 = (f32[24,8,128]{2,1,0:T(8,128)S(1)}, f32[24,8,128]{2,1,0:T(8,128)S(1)}, u32[]{:S(2)}, u32[]{:S(2)}) collective-permute-start(f32[24,8,128]{2,1,0:T(8,128)S(1)} %pad_maximum_fusion.2), channel_id=1, source_target_pairs={{1,0},{3,2},{5,4},{7,6},{9,8},{11,10},{13,12},{15,14},{17,16},{19,... | collective-permute-start | bytes 294920 | tf_op jit(solution)/shard_map/ppermute | solution.py:24
  87.1 1.6 %collective-permute-done.17.right_ref = f32[24,8,128]{2,1,0:T(8,128)S(1)} collective-permute-done((f32[24,8,128]{2,1,0:T(8,128)S(1)}, f32[24,8,128]{2,1,0:T(8,128)S(1)}, u32[]{:S(2)}, u32[]{:S(2)}) %collective-permute-start.17) | collective-permute-done | bytes 98336 | tf_op jit(solution)/shard_map/ppermute | solution.py:24
  88.7 0.7 broadcast_in_dim.30.kx_ref.refs_5_
  89.4 0.7 broadcast_in_dim.33.ky_ref.refs_6_
  90.1 9.1 %shard_map.58 = (f32[8,128,256]{2,1,0:T(8,128)}, f32[8,128,256]{2,1,0:T(8,128)}) custom-call(f32[8,128,128]{2,1,0:T(8,128)} %copy-done.7, f32[8,128,128]{2,1,0:T(8,128)} %copy-done.5, f32[8,128,128]{2,1,0:T(8,128)} %copy-done.6, f32[24,8,128]{2,1,0:T(8,128)} %copy-done.11, f32[24,8,128]{2,1,0:T(8,128)} %copy-done.12, ...), custom_call_target="tpu_custom_call" | custom-call | tf_op jit(solution)/shard_map/pallas_call | solution.py:155
  99.3 3.6 %collective-permute-done.12.refs_0_ = f32[8,144,128]{2,1,0:T(8,128)S(1)} collective-permute-done((f32[8,144,128]{2,1,0:T(8,128)S(1)}, f32[8,144,128]{2,1,0:T(8,128)S(1)}, u32[]{:S(2)}, u32[]{:S(2)}) %collective-permute-start.12) | collective-permute-done | bytes 589856 | tf_op jit(solution)/shard_map/ppermute | solution.py:24
  102.9 0.8 copy-done.8
  103.7 9.2 %shard_map.59 = (f32[8,128,256]{2,1,0:T(8,128)}, f32[8,128,256]{2,1,0:T(8,128)}) custom-call(f32[8,144,128]{2,1,0:T(8,128)} %copy-done.8, f32[8,128,128]{2,1,0:T(8,128)} %copy-done, f32[8,144,128]{2,1,0:T(8,128)} %collective-permute-done.13.refs_2_, f32[8,8,128]{2,1,0:T(8,128)} %copy-done.10, ...), custom_call_target="tpu_custom_call", output_to_operand_aliasing={{0}: (7, {}), {1}: (8, {})} | custom-call | tf_op jit(solution)/shard_map/pallas_call | solution.py:155
  (113 shorter events, 7.6 us)
Async XLA Ops:
  4.8 1.5 %collective-permute-start = (f32[32,1152]{1,0:T(8,128)S(1)}, f32[32,1152]{1,0:T(8,128)S(1)}, u32[]{:S(2)}, u32[]{:S(2)}) collective-permute-start(f32[32,1152]{1,0:T(8,128)S(1)} %concatenate.46), channel_id=1, source_target_pairs={{0,1},{1,0},{2,3},{3,2},{4,5},{5,4},{6,7},{7,6},{8,9},{9,8},{10,11... | collective-permute-start | bytes 442376 | tf_op jit(solution)/shard_map/ppermute | solution.py:78
  6.3 9.6 %collective-permute-start.3 = (f32[32,1152]{1,0:T(8,128)S(1)}, f32[32,1152]{1,0:T(8,128)S(1)}, u32[]{:S(2)}, u32[]{:S(2)}) collective-permute-start(f32[32,1152]{1,0:T(8,128)S(1)} %add.65), channel_id=1, source_target_pairs={{0,6},{2,4},{4,2},{6,0},{8,14},{10,12},{12,10},{14,8},{16,22},{18,... | collective-permute-start | bytes 442376 | tf_op jit(solution)/shard_map/ppermute | solution.py:75
  9.1 8.2 %collective-permute-start.2 = (f32[32,1152]{1,0:T(8,128)S(1)}, f32[32,1152]{1,0:T(8,128)S(1)}, u32[]{:S(2)}, u32[]{:S(2)}) collective-permute-start(f32[32,1152]{1,0:T(8,128)S(1)} %add.65), channel_id=1, source_target_pairs={{0,4},{2,6},{4,0},{6,2},{8,12},{10,14},{12,8},{14,10},{16,20},{18,... | collective-permute-start | bytes 442376 | tf_op jit(solution)/shard_map/ppermute | solution.py:75
  9.9 7.4 %collective-permute-start.1 = (f32[32,1152]{1,0:T(8,128)S(1)}, f32[32,1152]{1,0:T(8,128)S(1)}, u32[]{:S(2)}, u32[]{:S(2)}) collective-permute-start(f32[32,1152]{1,0:T(8,128)S(1)} %add.65), channel_id=1, source_target_pairs={{0,2},{2,0},{4,6},{6,4},{8,10},{10,8},{12,14},{14,12},{16,18},{18,... | collective-permute-start | bytes 442376 | tf_op jit(solution)/shard_map/ppermute | solution.py:75
  17.4 9.5 %collective-permute-start.6 = (f32[32,1152]{1,0:T(8,128)S(1)}, f32[32,1152]{1,0:T(8,128)S(1)}, u32[]{:S(2)}, u32[]{:S(2)}) collective-permute-start(f32[32,1152]{1,0:T(8,128)S(1)} %add_add_fusion.2), channel_id=1, source_target_pairs={{0,24},{2,26},{4,28},{6,30},{8,16},{10,18},{12,20},{14,22},{16,8},... | collective-permute-start | bytes 442376 | tf_op jit(solution)/shard_map/ppermute | solution.py:75
  21.5 7.6 %collective-permute-start.5 = (f32[32,1152]{1,0:T(8,128)S(1)}, f32[32,1152]{1,0:T(8,128)S(1)}, u32[]{:S(2)}, u32[]{:S(2)}) collective-permute-start(f32[32,1152]{1,0:T(8,128)S(1)} %add_add_fusion.2), channel_id=1, source_target_pairs={{0,16},{2,18},{4,20},{6,22},{8,24},{10,26},{12,28},{14,30},{16,0},... | collective-permute-start | bytes 442376 | tf_op jit(solution)/shard_map/ppermute | solution.py:75
  21.5 7.6 %collective-permute-start.4 = (f32[32,1152]{1,0:T(8,128)S(1)}, f32[32,1152]{1,0:T(8,128)S(1)}, u32[]{:S(2)}, u32[]{:S(2)}) collective-permute-start(f32[32,1152]{1,0:T(8,128)S(1)} %add_add_fusion.2), channel_id=1, source_target_pairs={{0,8},{2,10},{4,12},{6,14},{8,0},{10,2},{12,4},{14,6},{16,24},{18,... | collective-permute-start | bytes 442376 | tf_op jit(solution)/shard_map/ppermute | solution.py:75
  29.1 6.0 %collective-permute-start.9 = (f32[32,1152]{1,0:T(8,128)S(1)}, f32[32,1152]{1,0:T(8,128)S(1)}, u32[]{:S(2)}, u32[]{:S(2)}) collective-permute-start(f32[32,1152]{1,0:T(8,128)S(1)} %add_add_fusion.1), channel_id=1, source_target_pairs={{0,96},{2,98},{4,100},{6,102},{8,104},{10,106},{12,108},{14,110},{... | collective-permute-start | bytes 442376 | tf_op jit(solution)/shard_map/ppermute | solution.py:75
  30.7 6.6 %collective-permute-start.8 = (f32[32,1152]{1,0:T(8,128)S(1)}, f32[32,1152]{1,0:T(8,128)S(1)}, u32[]{:S(2)}, u32[]{:S(2)}) collective-permute-start(f32[32,1152]{1,0:T(8,128)S(1)} %add_add_fusion.1), channel_id=1, source_target_pairs={{0,64},{2,66},{4,68},{6,70},{8,72},{10,74},{12,76},{14,78},{16,80}... | collective-permute-start | bytes 442376 | tf_op jit(solution)/shard_map/ppermute | solution.py:75
  31.7 6.3 %collective-permute-start.7 = (f32[32,1152]{1,0:T(8,128)S(1)}, f32[32,1152]{1,0:T(8,128)S(1)}, u32[]{:S(2)}, u32[]{:S(2)}) collective-permute-start(f32[32,1152]{1,0:T(8,128)S(1)} %add_add_fusion.1), channel_id=1, source_target_pairs={{0,32},{2,34},{4,36},{6,38},{8,40},{10,42},{12,44},{14,46},{16,48}... | collective-permute-start | bytes 442376 | tf_op jit(solution)/shard_map/ppermute | solution.py:75
  38.0 0.7 copy-start.1
  40.7 0.8 slice-start
  54.0 1.2 %copy-start.4 = (bf16[8,128,256]{2,1,0:T(8,128)(2,1)S(1)}, bf16[8,128,256]{2,1,0:T(8,128)(2,1)}, u32[]{:S(2)}) copy-start(bf16[8,128,256]{2,1,0:T(8,128)(2,1)} %param.3) | copy-start | bytes 1572868
  54.3 1.3 %copy-start.2 = (f32[8,128,256]{2,1,0:T(8,128)S(1)}, f32[8,128,256]{2,1,0:T(8,128)}, u32[]{:S(2)}) copy-start(f32[8,128,256]{2,1,0:T(8,128)} %param.5) | copy-start | bytes 3145732
  54.3 1.6 %copy-start.3 = (f32[8,128,256]{2,1,0:T(8,128)S(1)}, f32[8,128,256]{2,1,0:T(8,128)}, u32[]{:S(2)}) copy-start(f32[8,128,256]{2,1,0:T(8,128)} %param.4) | copy-start | bytes 3145732
  57.6 15.2 %copy-start = (f32[8,128,128]{2,1,0:T(8,128)}, f32[8,128,128]{2,1,0:T(8,128)S(1)}, u32[]{:S(2)}) copy-start(f32[8,128,128]{2,1,0:T(8,128)S(1)} %get-tuple-element.16.refs_1_) | copy-start | bytes 1572868
  57.6 15.2 %copy-start.5 = (f32[8,128,128]{2,1,0:T(8,128)}, f32[8,128,128]{2,1,0:T(8,128)S(1)}, u32[]{:S(2)}) copy-start(f32[8,128,128]{2,1,0:T(8,128)S(1)} %get-tuple-element.15.mid_ref) | copy-start | bytes 1572868
  57.6 25.8 %collective-permute-start.15 = (f32[8,128,128]{2,1,0:T(8,128)S(1)}, f32[8,128,128]{2,1,0:T(8,128)S(1)}, u32[]{:S(2)}, u32[]{:S(2)}) collective-permute-start(f32[8,128,128]{2,1,0:T(8,128)S(1)} %get-tuple-element.15.mid_ref), channel_id=1, source_target_pairs={{2,0},{4,2},{6,4},{8,6},{10,8},{12,10},{14,12},{16,14},{18,16},{20... | collective-permute-start | bytes 1572872 | tf_op jit(solution)/shard_map/ppermute | solution.py:24
  65.6 17.8 %collective-permute-start.14 = (f32[8,128,128]{2,1,0:T(8,128)S(1)}, f32[8,128,128]{2,1,0:T(8,128)S(1)}, u32[]{:S(2)}, u32[]{:S(2)}) collective-permute-start(f32[8,128,128]{2,1,0:T(8,128)S(1)} %get-tuple-element.15.mid_ref), channel_id=1, source_target_pairs={{0,2},{2,4},{4,6},{6,8},{8,10},{10,12},{12,14},{14,16},{16,18},{18... | collective-permute-start | bytes 1572872 | tf_op jit(solution)/shard_map/ppermute | solution.py:24
  67.6 4.4 %collective-permute-start.11 = (f32[8,8,128]{2,1,0:T(8,128)S(1)}, f32[8,8,128]{2,1,0:T(8,128)S(1)}, u32[]{:S(2)}, u32[]{:S(2)}) collective-permute-start(f32[8,8,128]{2,1,0:T(8,128)S(1)} %get-tuple-element.13), channel_id=1, source_target_pairs={{1,0},{3,2},{5,4},{7,6},{9,8},{11,10},{13,12},{15,14},{17,16},{19,... | collective-permute-start | bytes 98312 | tf_op jit(solution)/shard_map/ppermute | solution.py:24
  68.9 3.9 %collective-permute-start.10 = (f32[8,8,128]{2,1,0:T(8,128)S(1)}, f32[8,8,128]{2,1,0:T(8,128)S(1)}, u32[]{:S(2)}, u32[]{:S(2)}) collective-permute-start(f32[8,8,128]{2,1,0:T(8,128)S(1)} %get-tuple-element.14), channel_id=1, source_target_pairs={{0,1},{2,3},{4,5},{6,7},{8,9},{10,11},{12,13},{14,15},{16,17},{18,... | collective-permute-start | bytes 98312 | tf_op jit(solution)/shard_map/ppermute | solution.py:24
  71.9 0.9 copy-start.9
  72.8 0.6 copy-start.10
  73.4 25.9 %collective-permute-start.13 = (f32[8,144,128]{2,1,0:T(8,128)S(1)}, f32[8,144,128]{2,1,0:T(8,128)}, u32[]{:S(2)}, u32[]{:S(2)}) collective-permute-start(f32[8,144,128]{2,1,0:T(8,128)S(1)} %pad_maximum_fusion), channel_id=1, source_target_pairs={{2,0},{4,2},{6,4},{8,6},{10,8},{12,10},{14,12},{16,14},{18,16},{20... | collective-permute-start | bytes 1769480 | tf_op jit(solution)/shard_map/ppermute | solution.py:24
  81.5 21.4 %collective-permute-start.12 = (f32[8,144,128]{2,1,0:T(8,128)S(1)}, f32[8,144,128]{2,1,0:T(8,128)S(1)}, u32[]{:S(2)}, u32[]{:S(2)}) collective-permute-start(f32[8,144,128]{2,1,0:T(8,128)S(1)} %pad_maximum_fusion), channel_id=1, source_target_pairs={{0,2},{2,4},{4,6},{6,8},{8,10},{10,12},{12,14},{14,16},{16,18},{18... | collective-permute-start | bytes 1769480 | tf_op jit(solution)/shard_map/ppermute | solution.py:24
  83.4 6.7 %copy-start.6 = (f32[8,128,128]{2,1,0:T(8,128)}, f32[8,128,128]{2,1,0:T(8,128)S(1)}, u32[]{:S(2)}) copy-start(f32[8,128,128]{2,1,0:T(8,128)S(1)} %collective-permute-done.15.down_ref) | copy-start | bytes 1572868
  83.5 6.7 %copy-start.7 = (f32[8,128,128]{2,1,0:T(8,128)}, f32[8,128,128]{2,1,0:T(8,128)S(1)}, u32[]{:S(2)}) copy-start(f32[8,128,128]{2,1,0:T(8,128)S(1)} %collective-permute-done.14.up_ref) | copy-start | bytes 1572868
  83.5 3.5 %collective-permute-start.16 = (f32[24,8,128]{2,1,0:T(8,128)S(1)}, f32[24,8,128]{2,1,0:T(8,128)S(1)}, u32[]{:S(2)}, u32[]{:S(2)}) collective-permute-start(f32[24,8,128]{2,1,0:T(8,128)S(1)} %pad_maximum_fusion.1), channel_id=1, source_target_pairs={{0,1},{2,3},{4,5},{6,7},{8,9},{10,11},{12,13},{14,15},{16,17},{18,... | collective-permute-start | bytes 294920 | tf_op jit(solution)/shard_map/ppermute | solution.py:24
  85.5 3.2 %collective-permute-start.17 = (f32[24,8,128]{2,1,0:T(8,128)S(1)}, f32[24,8,128]{2,1,0:T(8,128)S(1)}, u32[]{:S(2)}, u32[]{:S(2)}) collective-permute-start(f32[24,8,128]{2,1,0:T(8,128)S(1)} %pad_maximum_fusion.2), channel_id=1, source_target_pairs={{1,0},{3,2},{5,4},{7,6},{9,8},{11,10},{13,12},{15,14},{17,16},{19,... | collective-permute-start | bytes 294920 | tf_op jit(solution)/shard_map/ppermute | solution.py:24
  87.1 3.1 %copy-start.11 = (f32[24,8,128]{2,1,0:T(8,128)}, f32[24,8,128]{2,1,0:T(8,128)S(1)}, u32[]{:S(2)}) copy-start(f32[24,8,128]{2,1,0:T(8,128)S(1)} %collective-permute-done.16.left_ref) | copy-start | bytes 294916
  88.7 1.4 %copy-start.12 = (f32[24,8,128]{2,1,0:T(8,128)}, f32[24,8,128]{2,1,0:T(8,128)S(1)}, u32[]{:S(2)}) copy-start(f32[24,8,128]{2,1,0:T(8,128)S(1)} %collective-permute-done.17.right_ref) | copy-start | bytes 294916
  102.9 0.8 copy-start.8

commit v3 on v2

--- a/solution.py
+++ b/solution.py
@@ -82,14 +82,27 @@
 def summed_gram(flat):
     local = matmul(flat.T, flat)
     size = local.shape[0]
-    block = 32 if size % 32 == 0 else size
+    block = 32
     n = size // block
-    upper = [(i, j) for i in range(n) for j in range(i, n)]
-    packed = jnp.concatenate([local[i * block : (i + 1) * block, j * block : (j + 1) * block] for i, j in upper], axis=1)
-    packed = all_sum(packed)
-    piece = {ij: packed[:, k * block : (k + 1) * block] for k, ij in enumerate(upper)}
-    rows = [jnp.concatenate([piece[(i, j)] if i <= j else piece[(j, i)].T for j in range(n)], axis=1) for i in range(n)]
-    return jnp.concatenate(rows, axis=0)
+    if size % block or n % 2:
+        return all_sum(local)
+    packed = jnp.concatenate(
+        [
+            jnp.concatenate([local[k * block : (k + 1) * block, k * block :], local[size - (k + 1) * block : size - k * block, size - (k + 1) * block :]], axis=1)
+            for k in range(n // 2)
+        ],
+        axis=0,
+    )
+    packed = all_sum(packed.T).T
+    rows = [None] * n
+    for k in range(n // 2):
+        pair = packed[k * block : (k + 1) * block]
+        rows[k] = pair[:, : (n - k) * block]
+        rows[n - 1 - k] = pair[:, (n - k) * block :]
+    upper = jnp.concatenate([jnp.pad(r, ((0, 0), (size - r.shape[1], 0))) for r in rows], axis=0)
+    block_row = lax.broadcasted_iota(jnp.int32, (size, size), 0) // block
+    block_col = lax.broadcasted_iota(jnp.int32, (size, size), 1) // block
+    return jnp.where(block_row <= block_col, upper, upper.T)
 
 
 def tv_kernel(up_ref, mid_ref, down_ref, left_ref, right_ref, kx_ref, ky_ref, fg_ref, dual_ref, cols_first=False):

time: 113 us -> 115 us (1.018)
  waiting for transfers between devices: 25.6 us -> 31.6 us
  local copies, waits for them, and re-layouts: 7.98 us -> 4.08 us
    ppermute x9, waiting for transfers between devices: 18.2 us -> 24 us  [all_sum(): lax.ppermute(x, axis, [(i, i ^ k * step) for i in range(length)])]
    unnamed x58 -> x29, local copies, waits for them, and re-layouts: 4.32 us -> 1.66 us
where the time goes in v3:
time: 115 us
  starting transfers between devices  41.2 us (36%)
  waiting for transfers between devices  31.6 us (27%)
  Pallas kernels  18.3 us (16%)
  matrix products  15.8 us (14%)
  local copies, waits for them, and re-layouts  4.08 us (4%)
  between operations  2.64 us (2%)
  other arithmetic  1.2 us (1%)
    ppermute x8, starting transfers between devices, shifted(): return lax.ppermute(x, axis, pairs)  27.7 us
    ppermute x9, waiting for transfers between devices, all_sum(): lax.ppermute(x, axis, [(i, i ^ k * step) for i in range(length)])  24 us
    pallas_call x2, Pallas kernels, tv_local(): pl.pallas_call(body, grid=(1,), in_specs=in_specs, out_specs=[pl.BlockSpe...  18.3 us
    dot_general x39, matrix products, matmul(): jnp.dot(left, right, precision=lax.Precision.HIGH, preferred_element_type...  15.8 us
    ppermute x9, starting transfers between devices, all_sum(): lax.ppermute(x, axis, [(i, i ^ k * step) for i in range(length)])  13.4 us
    ppermute x8, waiting for transfers between devices, shifted(): return lax.ppermute(x, axis, pairs)  6.19 us
  transfers between devices with their start and end apart: 18, of which 11 were waited for; matrix products, arithmetic and copies ran while one was open for 1% of the time, Pallas kernels for 8%

profile of v3, /device:TPU:8, one launch (start us, length us, event | category | flops | bytes accessed | tf_op | source)
XLA Modules:
  0.0 114.9 jit_solution(7362843265220043260)
XLA Ops:
  0.6 3.5 %convolution_bitcast_fusion = f32[256,256]{1,0:T(8,128)S(1)} fusion(f32[8,128,256]{2,1,0:T(8,128)} %param.5, f32[8,128,256]{2,1,0:T(8,128)} %param.4, bf16[8,128,256]{2,1,0:T(8,128)(2,1)} %param.3), kind=kOutput, calls=%fused_computation.35 | convolution fusion | flops 403439616 | bytes 2883584 | tf_op jit(solution)/shard_map/dot_general | solution.py:28
  4.8 1.4 %collective-permute-done = f32[288,128]{0,1:T(8,128)S(1)} collective-permute-done((f32[288,128]{0,1:T(8,128)S(1)}, f32[288,128]{0,1:T(8,128)S(1)}, u32[]{:S(2)}, u32[]{:S(2)}) %collective-permute-start) | collective-permute-done | bytes 147488 | tf_op jit(solution)/shard_map/ppermute | solution.py:78
  6.4 2.8 %collective-permute-start.3 = (f32[288,128]{0,1:T(8,128)S(1)}, f32[288,128]{0,1:T(8,128)S(1)}, u32[]{:S(2)}, u32[]{:S(2)}) collective-permute-start(f32[288,128]{0,1:T(8,128)S(1)} %fusion.31), channel_id=1, source_target_pairs={{0,6},{2,4},{4,2},{6,0},{8,14},{10,12},{12,10},{14,8},{16,22},{18,... | collective-permute-start | bytes 442376 | tf_op jit(solution)/shard_map/ppermute | solution.py:75
  9.2 0.8 collective-permute-start.2
  10.0 0.5 collective-permute-start.1
  10.5 8.3 %collective-permute-done.3 = f32[288,128]{0,1:T(8,128)S(1)} collective-permute-done((f32[288,128]{0,1:T(8,128)S(1)}, f32[288,128]{0,1:T(8,128)S(1)}, u32[]{:S(2)}, u32[]{:S(2)}) %collective-permute-start.3) | collective-permute-done | bytes 147488 | tf_op jit(solution)/shard_map/ppermute | solution.py:75
  18.8 0.6 collective-permute-done.1
  19.5 4.1 %collective-permute-start.6 = (f32[288,128]{0,1:T(8,128)S(1)}, f32[288,128]{0,1:T(8,128)S(1)}, u32[]{:S(2)}, u32[]{:S(2)}) collective-permute-start(f32[288,128]{0,1:T(8,128)S(1)} %add_add_fusion.1), channel_id=1, source_target_pairs={{0,24},{2,26},{4,28},{6,30},{8,16},{10,18},{12,20},{14,22},{16,8},... | collective-permute-start | bytes 442376 | tf_op jit(solution)/shard_map/ppermute | solution.py:75
  23.6 0.9 collective-permute-start.4
  24.5 6.6 %collective-permute-done.6 = f32[288,128]{0,1:T(8,128)S(1)} collective-permute-done((f32[288,128]{0,1:T(8,128)S(1)}, f32[288,128]{0,1:T(8,128)S(1)}, u32[]{:S(2)}, u32[]{:S(2)}) %collective-permute-start.6) | collective-permute-done | bytes 147488 | tf_op jit(solution)/shard_map/ppermute | solution.py:75
  31.2 1.6 %collective-permute-done.5 = f32[288,128]{0,1:T(8,128)S(1)} collective-permute-done((f32[288,128]{0,1:T(8,128)S(1)}, f32[288,128]{0,1:T(8,128)S(1)}, u32[]{:S(2)}, u32[]{:S(2)}) %collective-permute-start.5) | collective-permute-done | bytes 147488 | tf_op jit(solution)/shard_map/ppermute | solution.py:75
  32.9 1.7 %collective-permute-start.9 = (f32[288,128]{0,1:T(8,128)S(1)}, f32[288,128]{0,1:T(8,128)S(1)}, u32[]{:S(2)}, u32[]{:S(2)}) collective-permute-start(f32[288,128]{0,1:T(8,128)S(1)} %add_add_fusion), channel_id=1, source_target_pairs={{0,96},{2,98},{4,100},{6,102},{8,104},{10,106},{12,108},{14,110},{... | collective-permute-start | bytes 442376 | tf_op jit(solution)/shard_map/ppermute | solution.py:75
  34.5 0.9 collective-permute-start.8
  35.5 1.6 %collective-permute-start.7 = (f32[288,128]{0,1:T(8,128)S(1)}, f32[288,128]{0,1:T(8,128)S(1)}, u32[]{:S(2)}, u32[]{:S(2)}) collective-permute-start(f32[288,128]{0,1:T(8,128)S(1)} %add_add_fusion), channel_id=1, source_target_pairs={{0,32},{2,34},{4,36},{6,38},{8,40},{10,42},{12,44},{14,46},{16,48}... | collective-permute-start | bytes 442376 | tf_op jit(solution)/shard_map/ppermute | solution.py:75
  37.1 4.5 %collective-permute-done.9 = f32[288,128]{0,1:T(8,128)S(1)} collective-permute-done((f32[288,128]{0,1:T(8,128)S(1)}, f32[288,128]{0,1:T(8,128)S(1)}, u32[]{:S(2)}, u32[]{:S(2)}) %collective-permute-start.9) | collective-permute-done | bytes 147488 | tf_op jit(solution)/shard_map/ppermute | solution.py:75
  41.6 1.2 %collective-permute-done.8 = f32[288,128]{0,1:T(8,128)S(1)} collective-permute-done((f32[288,128]{0,1:T(8,128)S(1)}, f32[288,128]{0,1:T(8,128)S(1)}, u32[]{:S(2)}, u32[]{:S(2)}) %collective-permute-start.8) | collective-permute-done | bytes 147488 | tf_op jit(solution)/shard_map/ppermute | solution.py:75
  42.7 1.1 collective-permute-done.7
  44.8 0.8 multiply_reduce_fusion
  46.5 0.3 fusion.28
  47.1 0.3 fusion.14
  47.4 0.3 fusion.37
  47.9 0.3 fusion.13
  48.8 0.3 fusion.12
  49.6 0.3 fusion.11
  49.9 0.3 fusion.43
  50.4 0.3 fusion.10
  50.7 0.3 fusion.45
  51.3 0.3 fusion.9
  51.5 0.3 fusion.47
  52.1 0.3 fusion.8
  52.4 0.9 select_reduce_fusion
  53.9 0.3 fusion.7
  54.2 0.3 fusion.20
  54.5 0.3 fusion.6
  54.8 0.3 fusion.48
  55.1 0.3 fusion.5
  55.3 0.3 fusion.49
  55.6 0.3 fusion.4
  55.9 0.3 fusion.50
  56.2 0.3 fusion.3
  56.5 0.3 fusion.51
  56.8 0.3 fusion.2
  57.1 0.3 fusion.52
  57.4 0.3 fusion.16
  57.6 0.3 fusion
  57.9 0.4 copy-done.1
  58.3 0.3 copy-done.2
  58.6 1.6 %fusion.18 = (f32[8,128,256]{2,1,0:T(8,128)S(1)}, f32[8,128,256]{2,1,0:T(8,128)}) fusion(f32[8,128,256]{2,1,0:T(8,128)S(1)} %copy-done.1, bf16[8,128,256]{2,1,0:T(8,128)(2,1)S(1)} %copy-done.3, f32[256,256,1]{1,0,2:T(8,128)S(1)} %fusion, f32[8,128,256]{2,1,0:T(8,128)S(1)} %copy-done.2), kind=kOutput, calls=%fused_computation.37 | convolution fusion | flops 404226048 | bytes 4980736 | tf_op jit(solution)/shard_map/dot_general | solution.py:28
  60.4 7.9 %collective-permute-start.15 = (f32[8,128,128]{2,1,0:T(8,128)S(1)}, f32[8,128,128]{2,1,0:T(8,128)S(1)}, u32[]{:S(2)}, u32[]{:S(2)}) collective-permute-start(f32[8,128,128]{2,1,0:T(8,128)S(1)} %get-tuple-element.17.mid_ref), channel_id=1, source_target_pairs={{2,0},{4,2},{6,4},{8,6},{10,8},{12,10},{14,12},{16,14},{18,16},{20... | collective-permute-start | bytes 1572872 | tf_op jit(solution)/shard_map/ppermute | solution.py:24
  68.3 1.9 %collective-permute-start.14 = (f32[8,128,128]{2,1,0:T(8,128)S(1)}, f32[8,128,128]{2,1,0:T(8,128)S(1)}, u32[]{:S(2)}, u32[]{:S(2)}) collective-permute-start(f32[8,128,128]{2,1,0:T(8,128)S(1)} %get-tuple-element.17.mid_ref), channel_id=1, source_target_pairs={{0,2},{2,4},{4,6},{6,8},{8,10},{10,12},{12,14},{14,16},{16,18},{18... | collective-permute-start | bytes 1572872 | tf_op jit(solution)/shard_map/ppermute | solution.py:24
  70.3 1.3 %collective-permute-start.11 = (f32[8,8,128]{2,1,0:T(8,128)S(1)}, f32[8,8,128]{2,1,0:T(8,128)S(1)}, u32[]{:S(2)}, u32[]{:S(2)}) collective-permute-start(f32[8,8,128]{2,1,0:T(8,128)S(1)} %get-tuple-element.15), channel_id=1, source_target_pairs={{1,0},{3,2},{5,4},{7,6},{9,8},{11,10},{13,12},{15,14},{17,16},{19,... | collective-permute-start | bytes 98312 | tf_op jit(solution)/shard_map/ppermute | solution.py:24
  71.6 3.0 %collective-permute-start.10 = (f32[8,8,128]{2,1,0:T(8,128)S(1)}, f32[8,8,128]{2,1,0:T(8,128)S(1)}, u32[]{:S(2)}, u32[]{:S(2)}) collective-permute-start(f32[8,8,128]{2,1,0:T(8,128)S(1)} %get-tuple-element.16), channel_id=1, source_target_pairs={{0,1},{2,3},{4,5},{6,7},{8,9},{10,11},{12,13},{14,15},{16,17},{18,... | collective-permute-start | bytes 98312 | tf_op jit(solution)/shard_map/ppermute | solution.py:24
  74.7 0.8 collective-permute-done.10.refs_3_
  75.5 0.5 copy-done.8
  76.1 8.1 %collective-permute-start.13 = (f32[8,144,128]{2,1,0:T(8,128)S(1)}, f32[8,144,128]{2,1,0:T(8,128)}, u32[]{:S(2)}, u32[]{:S(2)}) collective-permute-start(f32[8,144,128]{2,1,0:T(8,128)S(1)} %pad_maximum_fusion), channel_id=1, source_target_pairs={{2,0},{4,2},{6,4},{8,6},{10,8},{12,10},{14,12},{16,14},{18,16},{20... | collective-permute-start | bytes 1769480 | tf_op jit(solution)/shard_map/ppermute | solution.py:24
  84.2 1.9 %collective-permute-start.12 = (f32[8,144,128]{2,1,0:T(8,128)S(1)}, f32[8,144,128]{2,1,0:T(8,128)}, u32[]{:S(2)}, u32[]{:S(2)}) collective-permute-start(f32[8,144,128]{2,1,0:T(8,128)S(1)} %pad_maximum_fusion), channel_id=1, source_target_pairs={{0,2},{2,4},{4,6},{6,8},{8,10},{10,12},{12,14},{14,16},{16,18},{18... | collective-permute-start | bytes 1769480 | tf_op jit(solution)/shard_map/ppermute | solution.py:24
  86.2 2.0 %collective-permute-start.16 = (f32[24,8,128]{2,1,0:T(8,128)S(1)}, f32[24,8,128]{2,1,0:T(8,128)S(1)}, u32[]{:S(2)}, u32[]{:S(2)}) collective-permute-start(f32[24,8,128]{2,1,0:T(8,128)S(1)} %pad_maximum_fusion.1), channel_id=1, source_target_pairs={{0,1},{2,3},{4,5},{6,7},{8,9},{10,11},{12,13},{14,15},{16,17},{18,... | collective-permute-start | bytes 294920 | tf_op jit(solution)/shard_map/ppermute | solution.py:24
  88.2 1.5 %collective-permute-start.17 = (f32[24,8,128]{2,1,0:T(8,128)S(1)}, f32[24,8,128]{2,1,0:T(8,128)S(1)}, u32[]{:S(2)}, u32[]{:S(2)}) collective-permute-start(f32[24,8,128]{2,1,0:T(8,128)S(1)} %pad_maximum_fusion.2), channel_id=1, source_target_pairs={{1,0},{3,2},{5,4},{7,6},{9,8},{11,10},{13,12},{15,14},{17,16},{19,... | collective-permute-start | bytes 294920 | tf_op jit(solution)/shard_map/ppermute | solution.py:24
  89.8 1.6 %collective-permute-done.17.right_ref = f32[24,8,128]{2,1,0:T(8,128)S(1)} collective-permute-done((f32[24,8,128]{2,1,0:T(8,128)S(1)}, f32[24,8,128]{2,1,0:T(8,128)S(1)}, u32[]{:S(2)}, u32[]{:S(2)}) %collective-permute-start.17) | collective-permute-done | bytes 98336 | tf_op jit(solution)/shard_map/ppermute | solution.py:24
  91.4 0.7 broadcast_in_dim.30.kx_ref.refs_5_
  92.1 0.7 broadcast_in_dim.33.ky_ref.refs_6_
  92.8 9.1 %shard_map.58 = (f32[8,128,256]{2,1,0:T(8,128)}, f32[8,128,256]{2,1,0:T(8,128)}) custom-call(f32[8,128,128]{2,1,0:T(8,128)} %copy-done.6, f32[8,128,128]{2,1,0:T(8,128)} %copy-done.4, f32[8,128,128]{2,1,0:T(8,128)} %copy-done.5, f32[24,8,128]{2,1,0:T(8,128)} %copy-done.9, f32[24,8,128]{2,1,0:T(8,128)} %copy-done.10, ...), custom_call_target="tpu_custom_call" | custom-call | tf_op jit(solution)/shard_map/pallas_call | solution.py:168
  102.0 3.7 %collective-permute-done.12.refs_0_ = f32[8,144,128]{2,1,0:T(8,128)} collective-permute-done((f32[8,144,128]{2,1,0:T(8,128)S(1)}, f32[8,144,128]{2,1,0:T(8,128)}, u32[]{:S(2)}, u32[]{:S(2)}) %collective-permute-start.12) | collective-permute-done | bytes 589856 | tf_op jit(solution)/shard_map/ppermute | solution.py:24
  105.7 9.2 %shard_map.59 = (f32[8,128,256]{2,1,0:T(8,128)}, f32[8,128,256]{2,1,0:T(8,128)}) custom-call(f32[8,144,128]{2,1,0:T(8,128)} %collective-permute-done.12.refs_0_, f32[8,128,128]{2,1,0:T(8,128)} %copy-done, f32[8,144,128]{2,1,0:T(8,128)} %collective-permute-done.13.refs_2_, f32[8,8,128]{2,1,0:T(8,128)} %copy-done.8, ...), custom_call_target="tpu_custom_call", output_to_operand_aliasing={{0}: (7, {}), {1}: (8, {})} | custom-call | tf_op jit(solution)/shard_map/pallas_call | solution.py:168
  (78 shorter events, 4.6 us)
Async XLA Ops:
  4.7 1.5 %collective-permute-start = (f32[288,128]{0,1:T(8,128)S(1)}, f32[288,128]{0,1:T(8,128)S(1)}, u32[]{:S(2)}, u32[]{:S(2)}) collective-permute-start(f32[288,128]{0,1:T(8,128)S(1)} %maximum_bitcast_fusion), channel_id=1, source_target_pairs={{0,1},{1,0},{2,3},{3,2},{4,5},{5,4},{6,7},{7,6},{8,9},{9,8},{10,11... | collective-permute-start | bytes 442376 | tf_op jit(solution)/shard_map/ppermute | solution.py:78
  6.4 12.4 %collective-permute-start.3 = (f32[288,128]{0,1:T(8,128)S(1)}, f32[288,128]{0,1:T(8,128)S(1)}, u32[]{:S(2)}, u32[]{:S(2)}) collective-permute-start(f32[288,128]{0,1:T(8,128)S(1)} %fusion.31), channel_id=1, source_target_pairs={{0,6},{2,4},{4,2},{6,0},{8,14},{10,12},{12,10},{14,8},{16,22},{18,... | collective-permute-start | bytes 442376 | tf_op jit(solution)/shard_map/ppermute | solution.py:75
  9.2 9.6 %collective-permute-start.2 = (f32[288,128]{0,1:T(8,128)S(1)}, f32[288,128]{0,1:T(8,128)S(1)}, u32[]{:S(2)}, u32[]{:S(2)}) collective-permute-start(f32[288,128]{0,1:T(8,128)S(1)} %fusion.31), channel_id=1, source_target_pairs={{0,4},{2,6},{4,0},{6,2},{8,12},{10,14},{12,8},{14,10},{16,20},{18,... | collective-permute-start | bytes 442376 | tf_op jit(solution)/shard_map/ppermute | solution.py:75
  10.0 9.4 %collective-permute-start.1 = (f32[288,128]{0,1:T(8,128)S(1)}, f32[288,128]{0,1:T(8,128)S(1)}, u32[]{:S(2)}, u32[]{:S(2)}) collective-permute-start(f32[288,128]{0,1:T(8,128)S(1)} %fusion.31), channel_id=1, source_target_pairs={{0,2},{2,0},{4,6},{6,4},{8,10},{10,8},{12,14},{14,12},{16,18},{18,... | collective-permute-start | bytes 442376 | tf_op jit(solution)/shard_map/ppermute | solution.py:75
  19.5 11.7 %collective-permute-start.6 = (f32[288,128]{0,1:T(8,128)S(1)}, f32[288,128]{0,1:T(8,128)S(1)}, u32[]{:S(2)}, u32[]{:S(2)}) collective-permute-start(f32[288,128]{0,1:T(8,128)S(1)} %add_add_fusion.1), channel_id=1, source_target_pairs={{0,24},{2,26},{4,28},{6,30},{8,16},{10,18},{12,20},{14,22},{16,8},... | collective-permute-start | bytes 442376 | tf_op jit(solution)/shard_map/ppermute | solution.py:75
  23.6 9.2 %collective-permute-start.5 = (f32[288,128]{0,1:T(8,128)S(1)}, f32[288,128]{0,1:T(8,128)S(1)}, u32[]{:S(2)}, u32[]{:S(2)}) collective-permute-start(f32[288,128]{0,1:T(8,128)S(1)} %add_add_fusion.1), channel_id=1, source_target_pairs={{0,16},{2,18},{4,20},{6,22},{8,24},{10,26},{12,28},{14,30},{16,0},... | collective-permute-start | bytes 442376 | tf_op jit(solution)/shard_map/ppermute | solution.py:75
  23.6 9.2 %collective-permute-start.4 = (f32[288,128]{0,1:T(8,128)S(1)}, f32[288,128]{0,1:T(8,128)S(1)}, u32[]{:S(2)}, u32[]{:S(2)}) collective-permute-start(f32[288,128]{0,1:T(8,128)S(1)} %add_add_fusion.1), channel_id=1, source_target_pairs={{0,8},{2,10},{4,12},{6,14},{8,0},{10,2},{12,4},{14,6},{16,24},{18,... | collective-permute-start | bytes 442376 | tf_op jit(solution)/shard_map/ppermute | solution.py:75
  32.9 8.7 %collective-permute-start.9 = (f32[288,128]{0,1:T(8,128)S(1)}, f32[288,128]{0,1:T(8,128)S(1)}, u32[]{:S(2)}, u32[]{:S(2)}) collective-permute-start(f32[288,128]{0,1:T(8,128)S(1)} %add_add_fusion), channel_id=1, source_target_pairs={{0,96},{2,98},{4,100},{6,102},{8,104},{10,106},{12,108},{14,110},{... | collective-permute-start | bytes 442376 | tf_op jit(solution)/shard_map/ppermute | solution.py:75
  34.5 8.2 %collective-permute-start.8 = (f32[288,128]{0,1:T(8,128)S(1)}, f32[288,128]{0,1:T(8,128)S(1)}, u32[]{:S(2)}, u32[]{:S(2)}) collective-permute-start(f32[288,128]{0,1:T(8,128)S(1)} %add_add_fusion), channel_id=1, source_target_pairs={{0,64},{2,66},{4,68},{6,70},{8,72},{10,74},{12,76},{14,78},{16,80}... | collective-permute-start | bytes 442376 | tf_op jit(solution)/shard_map/ppermute | solution.py:75
  35.5 8.4 %collective-permute-start.7 = (f32[288,128]{0,1:T(8,128)S(1)}, f32[288,128]{0,1:T(8,128)S(1)}, u32[]{:S(2)}, u32[]{:S(2)}) collective-permute-start(f32[288,128]{0,1:T(8,128)S(1)} %add_add_fusion), channel_id=1, source_target_pairs={{0,32},{2,34},{4,36},{6,38},{8,40},{10,42},{12,44},{14,46},{16,48}... | collective-permute-start | bytes 442376 | tf_op jit(solution)/shard_map/ppermute | solution.py:75
  56.7 1.2 %copy-start.3 = (bf16[8,128,256]{2,1,0:T(8,128)(2,1)S(1)}, bf16[8,128,256]{2,1,0:T(8,128)(2,1)}, u32[]{:S(2)}) copy-start(bf16[8,128,256]{2,1,0:T(8,128)(2,1)} %param.3) | copy-start | bytes 1572868
  57.0 1.3 %copy-start.1 = (f32[8,128,256]{2,1,0:T(8,128)S(1)}, f32[8,128,256]{2,1,0:T(8,128)}, u32[]{:S(2)}) copy-start(f32[8,128,256]{2,1,0:T(8,128)} %param.5) | copy-start | bytes 3145732
  57.1 1.6 %copy-start.2 = (f32[8,128,256]{2,1,0:T(8,128)S(1)}, f32[8,128,256]{2,1,0:T(8,128)}, u32[]{:S(2)}) copy-start(f32[8,128,256]{2,1,0:T(8,128)} %param.4) | copy-start | bytes 3145732
  60.4 15.1 %copy-start = (f32[8,128,128]{2,1,0:T(8,128)}, f32[8,128,128]{2,1,0:T(8,128)S(1)}, u32[]{:S(2)}) copy-start(f32[8,128,128]{2,1,0:T(8,128)S(1)} %get-tuple-element.18.refs_1_) | copy-start | bytes 1572868
  60.4 15.1 %copy-start.4 = (f32[8,128,128]{2,1,0:T(8,128)}, f32[8,128,128]{2,1,0:T(8,128)S(1)}, u32[]{:S(2)}) copy-start(f32[8,128,128]{2,1,0:T(8,128)S(1)} %get-tuple-element.17.mid_ref) | copy-start | bytes 1572868
  60.4 25.8 %collective-permute-start.15 = (f32[8,128,128]{2,1,0:T(8,128)S(1)}, f32[8,128,128]{2,1,0:T(8,128)S(1)}, u32[]{:S(2)}, u32[]{:S(2)}) collective-permute-start(f32[8,128,128]{2,1,0:T(8,128)S(1)} %get-tuple-element.17.mid_ref), channel_id=1, source_target_pairs={{2,0},{4,2},{6,4},{8,6},{10,8},{12,10},{14,12},{16,14},{18,16},{20... | collective-permute-start | bytes 1572872 | tf_op jit(solution)/shard_map/ppermute | solution.py:24
  68.3 17.8 %collective-permute-start.14 = (f32[8,128,128]{2,1,0:T(8,128)S(1)}, f32[8,128,128]{2,1,0:T(8,128)S(1)}, u32[]{:S(2)}, u32[]{:S(2)}) collective-permute-start(f32[8,128,128]{2,1,0:T(8,128)S(1)} %get-tuple-element.17.mid_ref), channel_id=1, source_target_pairs={{0,2},{2,4},{4,6},{6,8},{8,10},{10,12},{12,14},{14,16},{16,18},{18... | collective-permute-start | bytes 1572872 | tf_op jit(solution)/shard_map/ppermute | solution.py:24
  70.3 4.4 %collective-permute-start.11 = (f32[8,8,128]{2,1,0:T(8,128)S(1)}, f32[8,8,128]{2,1,0:T(8,128)S(1)}, u32[]{:S(2)}, u32[]{:S(2)}) collective-permute-start(f32[8,8,128]{2,1,0:T(8,128)S(1)} %get-tuple-element.15), channel_id=1, source_target_pairs={{1,0},{3,2},{5,4},{7,6},{9,8},{11,10},{13,12},{15,14},{17,16},{19,... | collective-permute-start | bytes 98312 | tf_op jit(solution)/shard_map/ppermute | solution.py:24
  71.6 3.9 %collective-permute-start.10 = (f32[8,8,128]{2,1,0:T(8,128)S(1)}, f32[8,8,128]{2,1,0:T(8,128)S(1)}, u32[]{:S(2)}, u32[]{:S(2)}) collective-permute-start(f32[8,8,128]{2,1,0:T(8,128)S(1)} %get-tuple-element.16), channel_id=1, source_target_pairs={{0,1},{2,3},{4,5},{6,7},{8,9},{10,11},{12,13},{14,15},{16,17},{18,... | collective-permute-start | bytes 98312 | tf_op jit(solution)/shard_map/ppermute | solution.py:24
  74.6 0.9 copy-start.7
  75.5 0.6 copy-start.8
  76.1 25.9 %collective-permute-start.13 = (f32[8,144,128]{2,1,0:T(8,128)S(1)}, f32[8,144,128]{2,1,0:T(8,128)}, u32[]{:S(2)}, u32[]{:S(2)}) collective-permute-start(f32[8,144,128]{2,1,0:T(8,128)S(1)} %pad_maximum_fusion), channel_id=1, source_target_pairs={{2,0},{4,2},{6,4},{8,6},{10,8},{12,10},{14,12},{16,14},{18,16},{20... | collective-permute-start | bytes 1769480 | tf_op jit(solution)/shard_map/ppermute | solution.py:24
  84.2 21.5 %collective-permute-start.12 = (f32[8,144,128]{2,1,0:T(8,128)S(1)}, f32[8,144,128]{2,1,0:T(8,128)}, u32[]{:S(2)}, u32[]{:S(2)}) collective-permute-start(f32[8,144,128]{2,1,0:T(8,128)S(1)} %pad_maximum_fusion), channel_id=1, source_target_pairs={{0,2},{2,4},{4,6},{6,8},{8,10},{10,12},{12,14},{14,16},{16,18},{18... | collective-permute-start | bytes 1769480 | tf_op jit(solution)/shard_map/ppermute | solution.py:24
  86.1 6.7 %copy-start.5 = (f32[8,128,128]{2,1,0:T(8,128)}, f32[8,128,128]{2,1,0:T(8,128)S(1)}, u32[]{:S(2)}) copy-start(f32[8,128,128]{2,1,0:T(8,128)S(1)} %collective-permute-done.15.down_ref) | copy-start | bytes 1572868
  86.2 6.7 %copy-start.6 = (f32[8,128,128]{2,1,0:T(8,128)}, f32[8,128,128]{2,1,0:T(8,128)S(1)}, u32[]{:S(2)}) copy-start(f32[8,128,128]{2,1,0:T(8,128)S(1)} %collective-permute-done.14.up_ref) | copy-start | bytes 1572868
  86.2 3.5 %collective-permute-start.16 = (f32[24,8,128]{2,1,0:T(8,128)S(1)}, f32[24,8,128]{2,1,0:T(8,128)S(1)}, u32[]{:S(2)}, u32[]{:S(2)}) collective-permute-start(f32[24,8,128]{2,1,0:T(8,128)S(1)} %pad_maximum_fusion.1), channel_id=1, source_target_pairs={{0,1},{2,3},{4,5},{6,7},{8,9},{10,11},{12,13},{14,15},{16,17},{18,... | collective-permute-start | bytes 294920 | tf_op jit(solution)/shard_map/ppermute | solution.py:24
  88.2 3.2 %collective-permute-start.17 = (f32[24,8,128]{2,1,0:T(8,128)S(1)}, f32[24,8,128]{2,1,0:T(8,128)S(1)}, u32[]{:S(2)}, u32[]{:S(2)}) collective-permute-start(f32[24,8,128]{2,1,0:T(8,128)S(1)} %pad_maximum_fusion.2), channel_id=1, source_target_pairs={{1,0},{3,2},{5,4},{7,6},{9,8},{11,10},{13,12},{15,14},{17,16},{19,... | collective-permute-start | bytes 294920 | tf_op jit(solution)/shard_map/ppermute | solution.py:24
  89.8 3.1 %copy-start.9 = (f32[24,8,128]{2,1,0:T(8,128)}, f32[24,8,128]{2,1,0:T(8,128)S(1)}, u32[]{:S(2)}) copy-start(f32[24,8,128]{2,1,0:T(8,128)S(1)} %collective-permute-done.16.left_ref) | copy-start | bytes 294916
  91.4 1.4 %copy-start.10 = (f32[24,8,128]{2,1,0:T(8,128)}, f32[24,8,128]{2,1,0:T(8,128)S(1)}, u32[]{:S(2)}) copy-start(f32[24,8,128]{2,1,0:T(8,128)S(1)} %collective-permute-done.17.right_ref) | copy-start | bytes 294916

commit v4 on v2

--- a/solution.py
+++ b/solution.py
@@ -87,9 +87,15 @@
     upper = [(i, j) for i in range(n) for j in range(i, n)]
     packed = jnp.concatenate([local[i * block : (i + 1) * block, j * block : (j + 1) * block] for i, j in upper], axis=1)
     packed = all_sum(packed)
-    piece = {ij: packed[:, k * block : (k + 1) * block] for k, ij in enumerate(upper)}
-    rows = [jnp.concatenate([piece[(i, j)] if i <= j else piece[(j, i)].T for j in range(n)], axis=1) for i in range(n)]
-    return jnp.concatenate(rows, axis=0)
+    rows, start = [], 0
+    for i in range(n):
+        width = (n - i) * block
+        rows.append(jnp.pad(packed[:, start : start + width], ((0, 0), (size - width, 0))))
+        start += width
+    upper_part = jnp.concatenate(rows, axis=0)
+    block_row = lax.broadcasted_iota(jnp.int32, (size, size), 0) // block
+    block_col = lax.broadcasted_iota(jnp.int32, (size, size), 1) // block
+    return jnp.where(block_row <= block_col, upper_part, upper_part.T)
 
 
 def tv_kernel(up_ref, mid_ref, down_ref, left_ref, right_ref, kx_ref, ky_ref, fg_ref, dual_ref, cols_first=False):

time: 113 us -> 110 us (0.973)
  local copies, waits for them, and re-layouts: 7.98 us -> 4.42 us
    unnamed x58 -> x29, local copies, waits for them, and re-layouts: 4.32 us -> 1.66 us
where the time goes in v4:
time: 110 us; the launch traced here: 109 us
  starting transfers between devices  41.3 us (38%)
  waiting for transfers between devices  25.7 us (23%)
  Pallas kernels  18.3 us (17%)
  matrix products  15.8 us (14%)
  local copies, waits for them, and re-layouts  4.42 us (4%)
  between operations  2.61 us (2%)
    ppermute x8, starting transfers between devices, shifted(): return lax.ppermute(x, axis, pairs)  27.8 us
    pallas_call x2, Pallas kernels, tv_local(): pl.pallas_call(body, grid=(1,), in_specs=in_specs, out_specs=[pl.BlockSpe...  18.3 us
    ppermute x9, waiting for transfers between devices, all_sum(): lax.ppermute(x, axis, [(i, i ^ k * step) for i in range(length)])  18.2 us
    dot_general x39, matrix products, matmul(): jnp.dot(left, right, precision=lax.Precision.HIGH, preferred_element_type...  15.8 us
    ppermute x9, starting transfers between devices, all_sum(): lax.ppermute(x, axis, [(i, i ^ k * step) for i in range(length)])  13.4 us
    ppermute x8, waiting for transfers between devices, shifted(): return lax.ppermute(x, axis, pairs)  6.19 us
  transfers between devices with their start and end apart: 18, of which 11 were waited for; matrix products, arithmetic and copies ran while one was open for 1% of the time, Pallas kernels for 8%

profile of v4, /device:TPU:8, one launch (start us, length us, event | category | flops | bytes accessed | tf_op | source)
XLA Modules:
  0.0 109.2 jit_solution(4423240331477662843)
XLA Ops:
  0.6 3.5 %convolution_bitcast_fusion = f32[256,256]{1,0:T(8,128)S(1)} fusion(f32[8,128,256]{2,1,0:T(8,128)} %param.5, f32[8,128,256]{2,1,0:T(8,128)} %param.4, bf16[8,128,256]{2,1,0:T(8,128)(2,1)} %param.3), kind=kOutput, calls=%fused_computation.35 | convolution fusion | flops 403439616 | bytes 2883584 | tf_op jit(solution)/shard_map/dot_general | solution.py:28
  4.8 1.4 %collective-permute-done = f32[32,1152]{1,0:T(8,128)S(1)} collective-permute-done((f32[32,1152]{1,0:T(8,128)S(1)}, f32[32,1152]{1,0:T(8,128)S(1)}, u32[]{:S(2)}, u32[]{:S(2)}) %collective-permute-start) | collective-permute-done | bytes 147488 | tf_op jit(solution)/shard_map/ppermute | solution.py:78
  6.2 2.8 %collective-permute-start.3 = (f32[32,1152]{1,0:T(8,128)S(1)}, f32[32,1152]{1,0:T(8,128)S(1)}, u32[]{:S(2)}, u32[]{:S(2)}) collective-permute-start(f32[32,1152]{1,0:T(8,128)S(1)} %add.83), channel_id=1, source_target_pairs={{0,6},{2,4},{4,2},{6,0},{8,14},{10,12},{12,10},{14,8},{16,22},{18,... | collective-permute-start | bytes 442376 | tf_op jit(solution)/shard_map/ppermute | solution.py:75
  9.1 0.8 collective-permute-start.2
  9.9 0.5 collective-permute-start.1
  10.4 5.5 %collective-permute-done.3 = f32[32,1152]{1,0:T(8,128)S(1)} collective-permute-done((f32[32,1152]{1,0:T(8,128)S(1)}, f32[32,1152]{1,0:T(8,128)S(1)}, u32[]{:S(2)}, u32[]{:S(2)}) %collective-permute-start.3) | collective-permute-done | bytes 147488 | tf_op jit(solution)/shard_map/ppermute | solution.py:75
  15.9 1.4 %collective-permute-done.2 = f32[32,1152]{1,0:T(8,128)S(1)} collective-permute-done((f32[32,1152]{1,0:T(8,128)S(1)}, f32[32,1152]{1,0:T(8,128)S(1)}, u32[]{:S(2)}, u32[]{:S(2)}) %collective-permute-start.2) | collective-permute-done | bytes 147488 | tf_op jit(solution)/shard_map/ppermute | solution.py:75
  17.3 4.1 %collective-permute-start.6 = (f32[32,1152]{1,0:T(8,128)S(1)}, f32[32,1152]{1,0:T(8,128)S(1)}, u32[]{:S(2)}, u32[]{:S(2)}) collective-permute-start(f32[32,1152]{1,0:T(8,128)S(1)} %add_add_fusion.2), channel_id=1, source_target_pairs={{0,24},{2,26},{4,28},{6,30},{8,16},{10,18},{12,20},{14,22},{16,8},... | collective-permute-start | bytes 442376 | tf_op jit(solution)/shard_map/ppermute | solution.py:75
  21.4 0.9 collective-permute-start.4
  22.4 4.5 %collective-permute-done.6 = f32[32,1152]{1,0:T(8,128)S(1)} collective-permute-done((f32[32,1152]{1,0:T(8,128)S(1)}, f32[32,1152]{1,0:T(8,128)S(1)}, u32[]{:S(2)}, u32[]{:S(2)}) %collective-permute-start.6) | collective-permute-done | bytes 147488 | tf_op jit(solution)/shard_map/ppermute | solution.py:75
  26.9 2.1 %collective-permute-done.5 = f32[32,1152]{1,0:T(8,128)S(1)} collective-permute-done((f32[32,1152]{1,0:T(8,128)S(1)}, f32[32,1152]{1,0:T(8,128)S(1)}, u32[]{:S(2)}, u32[]{:S(2)}) %collective-permute-start.5) | collective-permute-done | bytes 147488 | tf_op jit(solution)/shard_map/ppermute | solution.py:75
  29.0 1.7 %collective-permute-start.9 = (f32[32,1152]{1,0:T(8,128)S(1)}, f32[32,1152]{1,0:T(8,128)S(1)}, u32[]{:S(2)}, u32[]{:S(2)}) collective-permute-start(f32[32,1152]{1,0:T(8,128)S(1)} %add_add_fusion.1), channel_id=1, source_target_pairs={{0,96},{2,98},{4,100},{6,102},{8,104},{10,106},{12,108},{14,110},{... | collective-permute-start | bytes 442376 | tf_op jit(solution)/shard_map/ppermute | solution.py:75
  30.7 0.9 collective-permute-start.8
  31.6 1.6 %collective-permute-start.7 = (f32[32,1152]{1,0:T(8,128)S(1)}, f32[32,1152]{1,0:T(8,128)S(1)}, u32[]{:S(2)}, u32[]{:S(2)}) collective-permute-start(f32[32,1152]{1,0:T(8,128)S(1)} %add_add_fusion.1), channel_id=1, source_target_pairs={{0,32},{2,34},{4,36},{6,38},{8,40},{10,42},{12,44},{14,46},{16,48}... | collective-permute-start | bytes 442376 | tf_op jit(solution)/shard_map/ppermute | solution.py:75
  33.2 1.8 %collective-permute-done.9 = f32[32,1152]{1,0:T(8,128)S(1)} collective-permute-done((f32[32,1152]{1,0:T(8,128)S(1)}, f32[32,1152]{1,0:T(8,128)S(1)}, u32[]{:S(2)}, u32[]{:S(2)}) %collective-permute-start.9) | collective-permute-done | bytes 147488 | tf_op jit(solution)/shard_map/ppermute | solution.py:75
  35.0 2.4 %collective-permute-done.8 = f32[32,1152]{1,0:T(8,128)S(1)} collective-permute-done((f32[32,1152]{1,0:T(8,128)S(1)}, f32[32,1152]{1,0:T(8,128)S(1)}, u32[]{:S(2)}, u32[]{:S(2)}) %collective-permute-start.8) | collective-permute-done | bytes 147488 | tf_op jit(solution)/shard_map/ppermute | solution.py:75
  37.3 0.6 collective-permute-done.7
  39.0 0.8 multiply_reduce_fusion
  40.8 0.3 fusion.28
  41.3 0.3 fusion.14
  41.6 0.3 fusion.36
  42.1 0.3 fusion.13
  43.0 0.3 fusion.12
  43.8 0.3 fusion.11
  44.1 0.3 fusion.42
  44.6 0.3 fusion.10
  44.9 0.3 fusion.44
  45.5 0.3 fusion.9
  45.8 0.3 fusion.46
  46.3 0.3 fusion.8
  46.6 0.9 select_reduce_fusion
  48.1 0.3 fusion.7
  48.4 0.3 fusion.20
  48.7 0.3 fusion.6
  49.0 0.3 fusion.47
  49.3 0.3 fusion.5
  49.6 0.3 fusion.48
  49.8 0.3 fusion.4
  50.1 0.3 fusion.49
  50.4 0.3 fusion.3
  50.7 0.3 fusion.50
  51.0 0.3 fusion.2
  51.3 0.3 fusion.51
  51.6 0.3 fusion.16
  51.9 0.3 fusion
  52.1 0.4 copy-done.1
  52.5 0.3 copy-done.2
  52.8 1.6 %fusion.18 = (f32[8,128,256]{2,1,0:T(8,128)S(1)}, f32[8,128,256]{2,1,0:T(8,128)}) fusion(f32[8,128,256]{2,1,0:T(8,128)S(1)} %copy-done.1, bf16[8,128,256]{2,1,0:T(8,128)(2,1)S(1)} %copy-done.3, f32[256,256,1]{1,0,2:T(8,128)S(1)} %fusion, f32[8,128,256]{2,1,0:T(8,128)S(1)} %copy-done.2), kind=kOutput, calls=%fused_computation.37 | convolution fusion | flops 404226048 | bytes 4980736 | tf_op jit(solution)/shard_map/dot_general | solution.py:28
  54.6 8.0 %collective-permute-start.15 = (f32[8,128,128]{2,1,0:T(8,128)S(1)}, f32[8,128,128]{2,1,0:T(8,128)S(1)}, u32[]{:S(2)}, u32[]{:S(2)}) collective-permute-start(f32[8,128,128]{2,1,0:T(8,128)S(1)} %get-tuple-element.17.mid_ref), channel_id=1, source_target_pairs={{2,0},{4,2},{6,4},{8,6},{10,8},{12,10},{14,12},{16,14},{18,16},{20... | collective-permute-start | bytes 1572872 | tf_op jit(solution)/shard_map/ppermute | solution.py:24
  62.6 1.9 %collective-permute-start.14 = (f32[8,128,128]{2,1,0:T(8,128)S(1)}, f32[8,128,128]{2,1,0:T(8,128)S(1)}, u32[]{:S(2)}, u32[]{:S(2)}) collective-permute-start(f32[8,128,128]{2,1,0:T(8,128)S(1)} %get-tuple-element.17.mid_ref), channel_id=1, source_target_pairs={{0,2},{2,4},{4,6},{6,8},{8,10},{10,12},{12,14},{14,16},{16,18},{18... | collective-permute-start | bytes 1572872 | tf_op jit(solution)/shard_map/ppermute | solution.py:24
  64.5 1.3 %collective-permute-start.11 = (f32[8,8,128]{2,1,0:T(8,128)S(1)}, f32[8,8,128]{2,1,0:T(8,128)S(1)}, u32[]{:S(2)}, u32[]{:S(2)}) collective-permute-start(f32[8,8,128]{2,1,0:T(8,128)S(1)} %get-tuple-element.15), channel_id=1, source_target_pairs={{1,0},{3,2},{5,4},{7,6},{9,8},{11,10},{13,12},{15,14},{17,16},{19,... | collective-permute-start | bytes 98312 | tf_op jit(solution)/shard_map/ppermute | solution.py:24
  65.8 3.0 %collective-permute-start.10 = (f32[8,8,128]{2,1,0:T(8,128)S(1)}, f32[8,8,128]{2,1,0:T(8,128)S(1)}, u32[]{:S(2)}, u32[]{:S(2)}) collective-permute-start(f32[8,8,128]{2,1,0:T(8,128)S(1)} %get-tuple-element.16), channel_id=1, source_target_pairs={{0,1},{2,3},{4,5},{6,7},{8,9},{10,11},{12,13},{14,15},{16,17},{18,... | collective-permute-start | bytes 98312 | tf_op jit(solution)/shard_map/ppermute | solution.py:24
  68.9 0.8 collective-permute-done.10.refs_3_
  69.8 0.5 copy-done.8
  70.3 8.1 %collective-permute-start.13 = (f32[8,144,128]{2,1,0:T(8,128)S(1)}, f32[8,144,128]{2,1,0:T(8,128)}, u32[]{:S(2)}, u32[]{:S(2)}) collective-permute-start(f32[8,144,128]{2,1,0:T(8,128)S(1)} %pad_maximum_fusion), channel_id=1, source_target_pairs={{2,0},{4,2},{6,4},{8,6},{10,8},{12,10},{14,12},{16,14},{18,16},{20... | collective-permute-start | bytes 1769480 | tf_op jit(solution)/shard_map/ppermute | solution.py:24
  78.5 1.9 %collective-permute-start.12 = (f32[8,144,128]{2,1,0:T(8,128)S(1)}, f32[8,144,128]{2,1,0:T(8,128)}, u32[]{:S(2)}, u32[]{:S(2)}) collective-permute-start(f32[8,144,128]{2,1,0:T(8,128)S(1)} %pad_maximum_fusion), channel_id=1, source_target_pairs={{0,2},{2,4},{4,6},{6,8},{8,10},{10,12},{12,14},{14,16},{16,18},{18... | collective-permute-start | bytes 1769480 | tf_op jit(solution)/shard_map/ppermute | solution.py:24
  80.5 2.0 %collective-permute-start.16 = (f32[24,8,128]{2,1,0:T(8,128)S(1)}, f32[24,8,128]{2,1,0:T(8,128)S(1)}, u32[]{:S(2)}, u32[]{:S(2)}) collective-permute-start(f32[24,8,128]{2,1,0:T(8,128)S(1)} %pad_maximum_fusion.1), channel_id=1, source_target_pairs={{0,1},{2,3},{4,5},{6,7},{8,9},{10,11},{12,13},{14,15},{16,17},{18,... | collective-permute-start | bytes 294920 | tf_op jit(solution)/shard_map/ppermute | solution.py:24
  82.5 1.5 %collective-permute-start.17 = (f32[24,8,128]{2,1,0:T(8,128)S(1)}, f32[24,8,128]{2,1,0:T(8,128)S(1)}, u32[]{:S(2)}, u32[]{:S(2)}) collective-permute-start(f32[24,8,128]{2,1,0:T(8,128)S(1)} %pad_maximum_fusion.2), channel_id=1, source_target_pairs={{1,0},{3,2},{5,4},{7,6},{9,8},{11,10},{13,12},{15,14},{17,16},{19,... | collective-permute-start | bytes 294920 | tf_op jit(solution)/shard_map/ppermute | solution.py:24
  84.0 1.6 %collective-permute-done.17.right_ref = f32[24,8,128]{2,1,0:T(8,128)S(1)} collective-permute-done((f32[24,8,128]{2,1,0:T(8,128)S(1)}, f32[24,8,128]{2,1,0:T(8,128)S(1)}, u32[]{:S(2)}, u32[]{:S(2)}) %collective-permute-start.17) | collective-permute-done | bytes 98336 | tf_op jit(solution)/shard_map/ppermute | solution.py:24
  85.7 0.7 broadcast_in_dim.30.kx_ref.refs_5_
  86.4 0.7 broadcast_in_dim.33.ky_ref.refs_6_
  87.1 9.1 %shard_map.58 = (f32[8,128,256]{2,1,0:T(8,128)}, f32[8,128,256]{2,1,0:T(8,128)}) custom-call(f32[8,128,128]{2,1,0:T(8,128)} %copy-done.6, f32[8,128,128]{2,1,0:T(8,128)} %copy-done.4, f32[8,128,128]{2,1,0:T(8,128)} %copy-done.5, f32[24,8,128]{2,1,0:T(8,128)} %copy-done.9, f32[24,8,128]{2,1,0:T(8,128)} %copy-done.10, ...), custom_call_target="tpu_custom_call" | custom-call | tf_op jit(solution)/shard_map/pallas_call | solution.py:161
  96.2 3.7 %collective-permute-done.12.refs_0_ = f32[8,144,128]{2,1,0:T(8,128)} collective-permute-done((f32[8,144,128]{2,1,0:T(8,128)S(1)}, f32[8,144,128]{2,1,0:T(8,128)}, u32[]{:S(2)}, u32[]{:S(2)}) %collective-permute-start.12) | collective-permute-done | bytes 589856 | tf_op jit(solution)/shard_map/ppermute | solution.py:24
  100.0 9.2 %shard_map.59 = (f32[8,128,256]{2,1,0:T(8,128)}, f32[8,128,256]{2,1,0:T(8,128)}) custom-call(f32[8,144,128]{2,1,0:T(8,128)} %collective-permute-done.12.refs_0_, f32[8,128,128]{2,1,0:T(8,128)} %copy-done, f32[8,144,128]{2,1,0:T(8,128)} %collective-permute-done.13.refs_2_, f32[8,8,128]{2,1,0:T(8,128)} %copy-done.8, ...), custom_call_target="tpu_custom_call", output_to_operand_aliasing={{0}: (7, {}), {1}: (8, {})} | custom-call | tf_op jit(solution)/shard_map/pallas_call | solution.py:161
  (78 shorter events, 4.7 us)
Async XLA Ops:
  4.7 1.5 %collective-permute-start = (f32[32,1152]{1,0:T(8,128)S(1)}, f32[32,1152]{1,0:T(8,128)S(1)}, u32[]{:S(2)}, u32[]{:S(2)}) collective-permute-start(f32[32,1152]{1,0:T(8,128)S(1)} %concatenate.17), channel_id=1, source_target_pairs={{0,1},{1,0},{2,3},{3,2},{4,5},{5,4},{6,7},{7,6},{8,9},{9,8},{10,11... | collective-permute-start | bytes 442376 | tf_op jit(solution)/shard_map/ppermute | solution.py:78
  6.2 9.6 %collective-permute-start.3 = (f32[32,1152]{1,0:T(8,128)S(1)}, f32[32,1152]{1,0:T(8,128)S(1)}, u32[]{:S(2)}, u32[]{:S(2)}) collective-permute-start(f32[32,1152]{1,0:T(8,128)S(1)} %add.83), channel_id=1, source_target_pairs={{0,6},{2,4},{4,2},{6,0},{8,14},{10,12},{12,10},{14,8},{16,22},{18,... | collective-permute-start | bytes 442376 | tf_op jit(solution)/shard_map/ppermute | solution.py:75
  9.1 8.2 %collective-permute-start.2 = (f32[32,1152]{1,0:T(8,128)S(1)}, f32[32,1152]{1,0:T(8,128)S(1)}, u32[]{:S(2)}, u32[]{:S(2)}) collective-permute-start(f32[32,1152]{1,0:T(8,128)S(1)} %add.83), channel_id=1, source_target_pairs={{0,4},{2,6},{4,0},{6,2},{8,12},{10,14},{12,8},{14,10},{16,20},{18,... | collective-permute-start | bytes 442376 | tf_op jit(solution)/shard_map/ppermute | solution.py:75
  9.9 7.4 %collective-permute-start.1 = (f32[32,1152]{1,0:T(8,128)S(1)}, f32[32,1152]{1,0:T(8,128)S(1)}, u32[]{:S(2)}, u32[]{:S(2)}) collective-permute-start(f32[32,1152]{1,0:T(8,128)S(1)} %add.83), channel_id=1, source_target_pairs={{0,2},{2,0},{4,6},{6,4},{8,10},{10,8},{12,14},{14,12},{16,18},{18,... | collective-permute-start | bytes 442376 | tf_op jit(solution)/shard_map/ppermute | solution.py:75
  17.3 9.5 %collective-permute-start.6 = (f32[32,1152]{1,0:T(8,128)S(1)}, f32[32,1152]{1,0:T(8,128)S(1)}, u32[]{:S(2)}, u32[]{:S(2)}) collective-permute-start(f32[32,1152]{1,0:T(8,128)S(1)} %add_add_fusion.2), channel_id=1, source_target_pairs={{0,24},{2,26},{4,28},{6,30},{8,16},{10,18},{12,20},{14,22},{16,8},... | collective-permute-start | bytes 442376 | tf_op jit(solution)/shard_map/ppermute | solution.py:75
  21.4 7.6 %collective-permute-start.5 = (f32[32,1152]{1,0:T(8,128)S(1)}, f32[32,1152]{1,0:T(8,128)S(1)}, u32[]{:S(2)}, u32[]{:S(2)}) collective-permute-start(f32[32,1152]{1,0:T(8,128)S(1)} %add_add_fusion.2), channel_id=1, source_target_pairs={{0,16},{2,18},{4,20},{6,22},{8,24},{10,26},{12,28},{14,30},{16,0},... | collective-permute-start | bytes 442376 | tf_op jit(solution)/shard_map/ppermute | solution.py:75
  21.4 7.6 %collective-permute-start.4 = (f32[32,1152]{1,0:T(8,128)S(1)}, f32[32,1152]{1,0:T(8,128)S(1)}, u32[]{:S(2)}, u32[]{:S(2)}) collective-permute-start(f32[32,1152]{1,0:T(8,128)S(1)} %add_add_fusion.2), channel_id=1, source_target_pairs={{0,8},{2,10},{4,12},{6,14},{8,0},{10,2},{12,4},{14,6},{16,24},{18,... | collective-permute-start | bytes 442376 | tf_op jit(solution)/shard_map/ppermute | solution.py:75
  29.0 6.0 %collective-permute-start.9 = (f32[32,1152]{1,0:T(8,128)S(1)}, f32[32,1152]{1,0:T(8,128)S(1)}, u32[]{:S(2)}, u32[]{:S(2)}) collective-permute-start(f32[32,1152]{1,0:T(8,128)S(1)} %add_add_fusion.1), channel_id=1, source_target_pairs={{0,96},{2,98},{4,100},{6,102},{8,104},{10,106},{12,108},{14,110},{... | collective-permute-start | bytes 442376 | tf_op jit(solution)/shard_map/ppermute | solution.py:75
  30.7 6.6 %collective-permute-start.8 = (f32[32,1152]{1,0:T(8,128)S(1)}, f32[32,1152]{1,0:T(8,128)S(1)}, u32[]{:S(2)}, u32[]{:S(2)}) collective-permute-start(f32[32,1152]{1,0:T(8,128)S(1)} %add_add_fusion.1), channel_id=1, source_target_pairs={{0,64},{2,66},{4,68},{6,70},{8,72},{10,74},{12,76},{14,78},{16,80}... | collective-permute-start | bytes 442376 | tf_op jit(solution)/shard_map/ppermute | solution.py:75
  31.6 6.3 %collective-permute-start.7 = (f32[32,1152]{1,0:T(8,128)S(1)}, f32[32,1152]{1,0:T(8,128)S(1)}, u32[]{:S(2)}, u32[]{:S(2)}) collective-permute-start(f32[32,1152]{1,0:T(8,128)S(1)} %add_add_fusion.1), channel_id=1, source_target_pairs={{0,32},{2,34},{4,36},{6,38},{8,40},{10,42},{12,44},{14,46},{16,48}... | collective-permute-start | bytes 442376 | tf_op jit(solution)/shard_map/ppermute | solution.py:75
  51.0 1.2 %copy-start.3 = (bf16[8,128,256]{2,1,0:T(8,128)(2,1)S(1)}, bf16[8,128,256]{2,1,0:T(8,128)(2,1)}, u32[]{:S(2)}) copy-start(bf16[8,128,256]{2,1,0:T(8,128)(2,1)} %param.3) | copy-start | bytes 1572868
  51.3 1.3 %copy-start.1 = (f32[8,128,256]{2,1,0:T(8,128)S(1)}, f32[8,128,256]{2,1,0:T(8,128)}, u32[]{:S(2)}) copy-start(f32[8,128,256]{2,1,0:T(8,128)} %param.5) | copy-start | bytes 3145732
  51.3 1.6 %copy-start.2 = (f32[8,128,256]{2,1,0:T(8,128)S(1)}, f32[8,128,256]{2,1,0:T(8,128)}, u32[]{:S(2)}) copy-start(f32[8,128,256]{2,1,0:T(8,128)} %param.4) | copy-start | bytes 3145732
  54.6 15.2 %copy-start = (f32[8,128,128]{2,1,0:T(8,128)}, f32[8,128,128]{2,1,0:T(8,128)S(1)}, u32[]{:S(2)}) copy-start(f32[8,128,128]{2,1,0:T(8,128)S(1)} %get-tuple-element.18.refs_1_) | copy-start | bytes 1572868
  54.6 15.2 %copy-start.4 = (f32[8,128,128]{2,1,0:T(8,128)}, f32[8,128,128]{2,1,0:T(8,128)S(1)}, u32[]{:S(2)}) copy-start(f32[8,128,128]{2,1,0:T(8,128)S(1)} %get-tuple-element.17.mid_ref) | copy-start | bytes 1572868
  54.6 25.8 %collective-permute-start.15 = (f32[8,128,128]{2,1,0:T(8,128)S(1)}, f32[8,128,128]{2,1,0:T(8,128)S(1)}, u32[]{:S(2)}, u32[]{:S(2)}) collective-permute-start(f32[8,128,128]{2,1,0:T(8,128)S(1)} %get-tuple-element.17.mid_ref), channel_id=1, source_target_pairs={{2,0},{4,2},{6,4},{8,6},{10,8},{12,10},{14,12},{16,14},{18,16},{20... | collective-permute-start | bytes 1572872 | tf_op jit(solution)/shard_map/ppermute | solution.py:24
  62.6 17.8 %collective-permute-start.14 = (f32[8,128,128]{2,1,0:T(8,128)S(1)}, f32[8,128,128]{2,1,0:T(8,128)S(1)}, u32[]{:S(2)}, u32[]{:S(2)}) collective-permute-start(f32[8,128,128]{2,1,0:T(8,128)S(1)} %get-tuple-element.17.mid_ref), channel_id=1, source_target_pairs={{0,2},{2,4},{4,6},{6,8},{8,10},{10,12},{12,14},{14,16},{16,18},{18... | collective-permute-start | bytes 1572872 | tf_op jit(solution)/shard_map/ppermute | solution.py:24
  64.5 4.4 %collective-permute-start.11 = (f32[8,8,128]{2,1,0:T(8,128)S(1)}, f32[8,8,128]{2,1,0:T(8,128)S(1)}, u32[]{:S(2)}, u32[]{:S(2)}) collective-permute-start(f32[8,8,128]{2,1,0:T(8,128)S(1)} %get-tuple-element.15), channel_id=1, source_target_pairs={{1,0},{3,2},{5,4},{7,6},{9,8},{11,10},{13,12},{15,14},{17,16},{19,... | collective-permute-start | bytes 98312 | tf_op jit(solution)/shard_map/ppermute | solution.py:24
  65.8 3.9 %collective-permute-start.10 = (f32[8,8,128]{2,1,0:T(8,128)S(1)}, f32[8,8,128]{2,1,0:T(8,128)S(1)}, u32[]{:S(2)}, u32[]{:S(2)}) collective-permute-start(f32[8,8,128]{2,1,0:T(8,128)S(1)} %get-tuple-element.16), channel_id=1, source_target_pairs={{0,1},{2,3},{4,5},{6,7},{8,9},{10,11},{12,13},{14,15},{16,17},{18,... | collective-permute-start | bytes 98312 | tf_op jit(solution)/shard_map/ppermute | solution.py:24
  68.9 0.9 copy-start.7
  69.7 0.6 copy-start.8
  70.3 25.9 %collective-permute-start.13 = (f32[8,144,128]{2,1,0:T(8,128)S(1)}, f32[8,144,128]{2,1,0:T(8,128)}, u32[]{:S(2)}, u32[]{:S(2)}) collective-permute-start(f32[8,144,128]{2,1,0:T(8,128)S(1)} %pad_maximum_fusion), channel_id=1, source_target_pairs={{2,0},{4,2},{6,4},{8,6},{10,8},{12,10},{14,12},{16,14},{18,16},{20... | collective-permute-start | bytes 1769480 | tf_op jit(solution)/shard_map/ppermute | solution.py:24
  78.5 21.5 %collective-permute-start.12 = (f32[8,144,128]{2,1,0:T(8,128)S(1)}, f32[8,144,128]{2,1,0:T(8,128)}, u32[]{:S(2)}, u32[]{:S(2)}) collective-permute-start(f32[8,144,128]{2,1,0:T(8,128)S(1)} %pad_maximum_fusion), channel_id=1, source_target_pairs={{0,2},{2,4},{4,6},{6,8},{8,10},{10,12},{12,14},{14,16},{16,18},{18... | collective-permute-start | bytes 1769480 | tf_op jit(solution)/shard_map/ppermute | solution.py:24
  80.4 6.7 %copy-start.5 = (f32[8,128,128]{2,1,0:T(8,128)}, f32[8,128,128]{2,1,0:T(8,128)S(1)}, u32[]{:S(2)}) copy-start(f32[8,128,128]{2,1,0:T(8,128)S(1)} %collective-permute-done.15.down_ref) | copy-start | bytes 1572868
  80.4 6.7 %copy-start.6 = (f32[8,128,128]{2,1,0:T(8,128)}, f32[8,128,128]{2,1,0:T(8,128)S(1)}, u32[]{:S(2)}) copy-start(f32[8,128,128]{2,1,0:T(8,128)S(1)} %collective-permute-done.14.up_ref) | copy-start | bytes 1572868
  80.5 3.5 %collective-permute-start.16 = (f32[24,8,128]{2,1,0:T(8,128)S(1)}, f32[24,8,128]{2,1,0:T(8,128)S(1)}, u32[]{:S(2)}, u32[]{:S(2)}) collective-permute-start(f32[24,8,128]{2,1,0:T(8,128)S(1)} %pad_maximum_fusion.1), channel_id=1, source_target_pairs={{0,1},{2,3},{4,5},{6,7},{8,9},{10,11},{12,13},{14,15},{16,17},{18,... | collective-permute-start | bytes 294920 | tf_op jit(solution)/shard_map/ppermute | solution.py:24
  82.5 3.2 %collective-permute-start.17 = (f32[24,8,128]{2,1,0:T(8,128)S(1)}, f32[24,8,128]{2,1,0:T(8,128)S(1)}, u32[]{:S(2)}, u32[]{:S(2)}) collective-permute-start(f32[24,8,128]{2,1,0:T(8,128)S(1)} %pad_maximum_fusion.2), channel_id=1, source_target_pairs={{1,0},{3,2},{5,4},{7,6},{9,8},{11,10},{13,12},{15,14},{17,16},{19,... | collective-permute-start | bytes 294920 | tf_op jit(solution)/shard_map/ppermute | solution.py:24
  84.0 3.1 %copy-start.9 = (f32[24,8,128]{2,1,0:T(8,128)}, f32[24,8,128]{2,1,0:T(8,128)S(1)}, u32[]{:S(2)}) copy-start(f32[24,8,128]{2,1,0:T(8,128)S(1)} %collective-permute-done.16.left_ref) | copy-start | bytes 294916
  85.7 1.4 %copy-start.10 = (f32[24,8,128]{2,1,0:T(8,128)}, f32[24,8,128]{2,1,0:T(8,128)S(1)}, u32[]{:S(2)}) copy-start(f32[24,8,128]{2,1,0:T(8,128)S(1)} %collective-permute-done.17.right_ref) | copy-start | bytes 294916
